TPU v7x, 32 devices: a whole 2x2x4 slice. The times are simulated.
32 devices in a mesh: span: 4 (over z), wall: 8 (over y, x, core).
Axes of the slice: x: 2, y: 2, z: 4, core: 2. Of those that a mesh axis runs over, the one named last changes fastest.
Arguments:
- random_field: bfloat16 [64, 1536, 4096], P(None, 'wall', 'span'), may hold values from -64 to 64
- half_widths: int32 [2, 1536], replicated, may hold values from 2 to 128, as said below
- time_scale: float32 [1536], P('wall'), may hold values from 4 to 64
- target_rms: float32 [1536], P('wall'), may hold values from 0.2 to 2
- previous_state: float32 [1536, 4096], P('wall', 'span'), may hold values from -4 to 4
Outputs:
- inflow: float32 [64, 1536, 4096], P(None, 'wall', 'span')
- final_state: float32 [1536, 4096], P('wall', 'span')
Inputs may be any that keep to these rules, and one draw needn't show every extreme that they name: `half_widths`: row 0 holds each row's wall-normal half-width and row 1 its spanwise one; both rows reach 128.
All inputs are finite; a program needn't handle non-finite values.
Results may differ from a plain program's by a relative error of at most 0.005.
The roundings to bfloat16 on the way count: a program that leaves them out, or rounds other values in their place, can miss the bound.
Values may be sent and summed in bfloat16 or wider, within the bound.
No kernel may reach another device: no remote copies, remote signals or barrier semaphores. Data moves between devices by JAX's collectives and lax.ppermute only.
A program may use at most 256 MiB of HBM per device.

v0:
```python
import math

import jax
import jax.numpy as jnp
from jax import lax
from jax.sharding import PartitionSpec as P

NZ = 4096
MAXW = 128


def extended_2(cells, sides, width):
    for axis, dim in sides:
        count = lax.axis_size(axis)
        head = lax.slice_in_dim(cells, 0, width, axis=dim)
        tail = lax.slice_in_dim(cells, cells.shape[dim] - width, cells.shape[dim], axis=dim)
        cells = jnp.concatenate(
            [
                lax.ppermute(tail, axis, [(i, (i + 1) % count) for i in range(count)]),
                cells,
                lax.ppermute(head, axis, [((i + 1) % count, i) for i in range(count)]),
            ],
            axis=dim,
        )
    return cells


def passed_along(array, axis, by):
    length = lax.axis_size(axis)
    pairs = [(i, i + by) for i in range(length) if 0 <= i + by < length]
    return lax.ppermute(array, axis, pairs)


def kernel_norm(half_width):
    spread = jnp.arange(-MAXW, MAXW + 1).astype(jnp.float32)
    widths_f = half_width.astype(jnp.float32)[:, None]
    inside = jnp.abs(spread)[None, :] <= widths_f
    terms = jnp.where(inside, jnp.exp(-math.pi * spread * spread / (widths_f * widths_f)), 0.0)
    return jnp.sqrt(jnp.sum(terms, axis=1))


def kernel_values(half_width, norm_rows, offsets):
    extra = (1,) * (offsets.ndim - 1)
    widths_f = half_width.astype(jnp.float32).reshape(half_width.shape + extra)
    scaled = norm_rows.reshape(norm_rows.shape + extra)
    values = jnp.where(
        jnp.abs(offsets) <= widths_f,
        jnp.exp(-0.5 * math.pi * offsets * offsets / (widths_f * widths_f)) / scaled,
        0.0,
    )
    return values.astype(jnp.bfloat16)


def wall_matrix(half_all, first_row, row_count):
    offsets = (
        jnp.arange(row_count + 2 * MAXW)[None, :] - jnp.arange(row_count)[:, None] - MAXW
    ).astype(jnp.float32)
    halves = lax.dynamic_slice_in_dim(half_all, first_row, row_count)
    return kernel_values(halves, kernel_norm(halves), offsets)


def combine(earlier, later):
    return (earlier[0] * later[0], later[0] * earlier[1] + later[1])


def body(random_field, half_widths, time_scale, target_rms, previous_state):
    planes, row_count, col_count = random_field.shape
    first_row = lax.axis_index("wall") * row_count
    wall_half = half_widths[0]
    span_local = lax.dynamic_slice_in_dim(half_widths[1], first_row, row_count)
    extended = extended_2(random_field, (("span", 2),), MAXW)
    row_block = math.gcd(row_count, 8)
    block_count = row_count // row_block
    span_cols = col_count + 2 * MAXW
    offsets = (jnp.arange(span_cols)[:, None] - jnp.arange(col_count)[None, :] - MAXW).astype(
        jnp.float32
    )
    norm_local = kernel_norm(span_local)
    by_row = jnp.transpose(extended, (1, 0, 2)).reshape(block_count, row_block, planes, span_cols)

    def span_block(packed):
        noise_rows, half_width, norm_row = packed
        matrix = kernel_values(
            half_width, norm_row, jnp.broadcast_to(offsets, (row_block,) + offsets.shape)
        )
        return jnp.einsum(
            "yjz,ypj->ypz", matrix, noise_rows, preferred_element_type=jnp.float32
        ).astype(jnp.bfloat16)

    spanned = lax.map(
        span_block,
        (
            by_row,
            span_local.reshape(block_count, row_block),
            norm_local.reshape(block_count, row_block),
        ),
    )
    spanned = jnp.transpose(spanned.reshape(row_count, planes, col_count), (1, 0, 2))
    reach_steps = -(-MAXW // row_count)
    lower_rims = []
    upper_rims = []
    for distance in range(1, reach_steps + 1):
        rim_rows = min(row_count, MAXW - (distance - 1) * row_count)
        lower_rims.insert(0, passed_along(spanned[:, row_count - rim_rows :], "wall", distance))
        upper_rims.append(passed_along(spanned[:, :rim_rows], "wall", -distance))
    window = jnp.concatenate(lower_rims + [spanned] + upper_rims, axis=1)
    matrix = wall_matrix(wall_half, first_row, row_count)
    filtered = jnp.einsum("yk,pkz->pyz", matrix, window, preferred_element_type=jnp.float32).astype(
        jnp.bfloat16
    )
    decay_rate = jnp.exp(-math.pi / (2.0 * time_scale))[:, None]
    noise_gain = jnp.sqrt(1.0 - jnp.exp(-math.pi / time_scale))[:, None]
    driven = noise_gain[None] * filtered.astype(jnp.float32)
    driven = jnp.concatenate(
        [driven[:1] + decay_rate[None] * previous_state[None], driven[1:]], axis=0
    )
    factors = jnp.broadcast_to(decay_rate[None], (planes, row_count, 1))
    _, states = lax.associative_scan(combine, (factors, driven), axis=0)
    energy = lax.psum(jnp.sum(states * states, axis=2), "span")
    row_scale = target_rms[None, :] / jnp.sqrt(energy / NZ + 1e-06)
    inflow = states * row_scale[:, :, None]
    return (inflow, states[-1])


def solution(mesh):
    in_specs = (P(None, "wall", "span"), P(), P("wall"), P("wall"), P("wall", "span"))
    out_specs = (P(None, "wall", "span"), P("wall", "span"))
    return jax.shard_map(body, mesh=mesh, in_specs=in_specs, out_specs=out_specs, check_vma=False)
```

profile of v0, /device:TPU:4, one launch (start us, length us, event | category | flops | bytes accessed | tf_op | source)
XLA Modules:
  0.0 1488.5 jit_solution(14588355432185727975)
XLA Ops:
  10.6 68.2 %collective-permute-done = bf16[64,192,128]{2,1,0:T(8,128)(2,1)} collective-permute-done((bf16[64,192,128]{2,1,0:T(8,128)(2,1)}, bf16[64,192,128]{2,1,0:T(8,128)(2,1)}, u32[]{:S(2)}, u32[]{:S(2)}) %collective-permute-start) | collective-permute-done | bytes 3145760 | tf_op jit(solution)/shard_map/ppermute | solution.py:19
  78.7 65.5 %collective-permute-done.1 = bf16[64,192,128]{2,1,0:T(8,128)(2,1)} collective-permute-done((bf16[64,192,128]{2,1,0:T(8,128)(2,1)S(1)}, bf16[64,192,128]{2,1,0:T(8,128)(2,1)}, u32[]{:S(2)}, u32[]{:S(2)}) %collective-permute-start.1) | collective-permute-done | bytes 3145760 | tf_op jit(solution)/shard_map/ppermute | solution.py:21
  144.3 21.7 %maximum_bitcast_fusion = bf16[192,64,1280]{2,0,1:T(8,128)(2,1)} fusion(bf16[64,192,128]{2,1,0:T(8,128)(2,1)} %collective-permute-done.1, bf16[64,192,1024]{2,1,0:T(8,128)(2,1)} %param.7, bf16[64,192,128]{2,1,0:T(8,128)(2,1)} %collective-permute-done), kind=kLoop, calls=%fused_computation.31 | loop fusion | flops 94371840 | bytes 62914560 | tf_op jit(solution)/shard_map/transpose | solution.py:79
  166.0 29.6 %copy.11 = bf16[192,64,1280]{2,1,0:T(8,128)(2,1)} copy(bf16[192,64,1280]{2,0,1:T(8,128)(2,1)} %maximum_bitcast_fusion) | data formatting | bytes 62914560 | tf_op jit(solution)/shard_map/transpose | solution.py:79
  195.6 329.2 %while.12 = (s32[]{:T(128)}, bf16[24,8,64,1024]{3,1,0,2:T(8,128)(2,1)}, bf16[24,8,64,1280]{3,2,1,0:T(8,128)(2,1)}, s32[24,8]{1,0:T(8,128)S(1)}, f32[24,8]{1,0:T(8,128)S(1)}, /*index=5*/s32[]{:T(128)}) while((s32[]{:T(128)}, bf16[24,8,64,1024]{3,1,0,2:T(8,128)(2,1)}, bf16[24,8,64,1280]{3,2,1,0:T(8,128)(2,1)}, ...), condition=%wide.region_2.3_spmd.clone, body=%wide.region_1.2_spmd.clone.sunk | while | flops 1402994688 | bytes 25428316 | solution.py:90
  197.2 10.6 fusion.80
  210.9 10.6 fusion.80
  224.6 10.6 fusion.80
  238.3 10.6 fusion.80
  252.0 10.6 fusion.80
  265.7 10.6 fusion.80
  279.4 10.6 fusion.80
  293.2 10.6 fusion.80
  306.9 10.6 fusion.80
  320.7 10.6 fusion.80
  334.4 10.6 fusion.80
  348.1 10.6 fusion.80
  361.9 10.6 fusion.80
  375.6 10.6 fusion.80
  389.3 10.6 fusion.80
  416.7 10.6 fusion.80
  430.4 10.6 fusion.80
  444.1 10.6 fusion.80
  457.8 10.6 fusion.80
  471.5 10.6 fusion.80
  485.2 10.6 fusion.80
  512.6 10.6 fusion.80
  524.8 12.9 fusion.63
  545.5 354.7 %collective-permute-done.2 = bf16[64,128,1024]{2,1,0:T(8,128)(2,1)S(1)} collective-permute-done((bf16[64,128,1024]{2,1,0:T(8,128)(2,1)S(1)}, bf16[64,128,1024]{2,1,0:T(8,128)(2,1)S(1)}, u32[]{:S(2)}, u32[]{:S(2)}) %collective-permute-start.2) | collective-permute-done | bytes 16777248 | tf_op jit(solution)/shard_map/ppermute | solution.py:31
  906.0 38.7 %multiply_bitcast_fusion = f32[64,192,1024]{2,1,0:T(8,128)} fusion(f32[192]{0:T(256)S(1)} %get-tuple-element.113, bf16[64,128,1024]{2,1,0:T(8,128)(2,1)} %collective-permute-done.3, bf16[64,192,1024]{2,1,0:T(8,128)(2,1)} %bitcast.39, bf16[64,128,1024]{2,1,0:T(8,128)(2,1)} %copy-done.20, f32[192]{0:T(256)S(1)} %sqrt.23, f32[192]{0:T(256)S(1)} %copy-done.17, ...), kind=kOutput, calls=%fused_computation.30 | convolution fusion | flops 11489144832 | bytes 109054976 | tf_op jit(solution)/shard_map/yk,pkz->pyz/dot_general | solution.py:108
  944.7 35.1 %slice.163 = f32[63,192,1024]{2,1,0:T(8,128)} slice(f32[64,192,1024]{2,1,0:T(8,128)} %multiply_bitcast_fusion), slice={[1:64], [0:192], [0:1024]} | slice | bytes 99090432 | tf_op jit(solution)/shard_map/slice | solution.py:115
  981.1 35.1 %pad_maximum_fusion = f32[64,192,1024]{2,1,0:T(8,128)} fusion(f32[63,192,1024]{2,1,0:T(8,128)} %slice.163, f32[1,192,1024]{2,1,0:T(8,128)S(1)} %slice_add_fusion.6), kind=kLoop, calls=%fused_computation.28 | loop fusion | flops 12582912 | bytes 100663296 | tf_op jit(solution)/shard_map/concatenate | solution.py:114
  1016.1 16.7 %slice_add_fusion = f32[32,192,1024]{2,1,0:T(8,128)S(1)} fusion(f32[63,192,1024]{2,1,0:T(8,128)} %slice.163, f32[64,192,1024]{2,1,0:T(8,128)} %pad_maximum_fusion, f32[192]{0:T(256)S(1)} %get-tuple-element.94), kind=kLoop, calls=%fused_computation.34 | loop fusion | flops 12582912 | bytes 75498240 | tf_op jit(solution)/shard_map/add | solution.py:63
  1088.1 11.2 fusion.32
  1109.5 12.4 pad.43
  1121.9 12.4 pad.44
  1134.3 18.0 %fusion.31 = f32[15,192,1024]{2,1,0:T(8,128)} fusion(f32[16,192,1024]{2,1,0:T(8,128)} %pad.44, f32[16,192,1024]{2,1,0:T(8,128)} %pad.43, f32[32,192,1024]{2,1,0:T(8,128)} %copy-done, f32[192]{0:T(256)S(1)} %get-tuple-element.110), kind=kLoop, calls=%fused_computation.40 | loop fusion | flops 8847360 | bytes 47186688 | tf_op jit(solution)/shard_map/add | solution.py:63
  1153.0 11.4 add.128
  1164.4 11.8 pad_maximum_fusion.2
  1176.2 23.3 %pad.45 = f32[32,192,1024]{2,1,0:T(8,128)} pad(f32[16,192,1024]{2,1,0:T(8,128)} %pad_maximum_fusion.2, f32[]{:T(128)} %constant.54.clone.1), padding=0_1_1x0_0_0x0_0_0 | pad | bytes 37748740 | tf_op jit(solution)/shard_map/pad | solution.py:118
  1199.5 23.3 %pad.46 = f32[32,192,1024]{2,1,0:T(8,128)} pad(f32[16,192,1024]{2,1,0:T(8,128)} %add.128, f32[]{:T(128)} %constant.54.clone.1), padding=1_0_1x0_0_0x0_0_0 | pad | bytes 37748740 | tf_op jit(solution)/shard_map/pad | solution.py:118
  1222.8 32.9 %fusion.28 = f32[31,192,1024]{2,1,0:T(8,128)} fusion(f32[32,192,1024]{2,1,0:T(8,128)} %pad.46, f32[32,192,1024]{2,1,0:T(8,128)} %pad.45, f32[63,192,1024]{2,1,0:T(8,128)} %slice.163, f32[192]{0:T(256)S(1)} %get-tuple-element.94), kind=kLoop, calls=%fused_computation.36 | loop fusion | flops 18284544 | bytes 97518336 | tf_op jit(solution)/shard_map/add | solution.py:63
  1255.7 27.0 %add.130 = f32[32,192,1024]{2,1,0:T(8,128)} add(f32[32,192,1024]{2,1,0:T(8,128)} %pad.45, f32[32,192,1024]{2,1,0:T(8,128)} %pad.46) | non-fusion elementwise | flops 6291456 | bytes 75497472 | tf_op jit(solution)/shard_map/add | solution.py:118
  1295.8 45.3 %pad.47 = f32[64,192,1024]{2,1,0:T(8,128)} pad(f32[32,192,1024]{2,1,0:T(8,128)} %pad_maximum_fusion.1, f32[]{:T(128)} %constant.54.clone.1), padding=0_1_1x0_0_0x0_0_0 | pad | bytes 75497472 | tf_op jit(solution)/shard_map/pad | solution.py:118
  1341.1 45.3 %pad.48 = f32[64,192,1024]{2,1,0:T(8,128)} pad(f32[32,192,1024]{2,1,0:T(8,128)} %add.130, f32[]{:T(128)} %constant.54.clone.1), padding=1_0_1x0_0_0x0_0_0 | pad | bytes 75497472 | tf_op jit(solution)/shard_map/pad | solution.py:118
  1388.8 48.0 %multiply_reduce_fusion = (f32[64,192]{1,0:T(8,128)S(1)}, f32[64,192,1024]{2,1,0:T(8,128)}) fusion(f32[64,192,1024]{2,1,0:T(8,128)} %pad.47, f32[64,192,1024]{2,1,0:T(8,128)} %pad.48), kind=kLoop, calls=%fused_computation.29 | loop fusion | flops 37736448 | bytes 151044096 | tf_op jit(solution)/shard_map/reduce_sum | solution.py:119
  1436.8 18.8 %psum.7 = f32[64,192]{1,0:T(8,128)S(1)} all-reduce(f32[64,192]{1,0:T(8,128)S(1)} %get-tuple-element.91), channel_id=1, replica_groups=mesh['span'=4,'wall'=8] {'span'}, use_global_device_ids=true, to_apply=%region_5.6 | all-reduce | flops 12288 | bytes 98304 | tf_op jit(solution)/shard_map/psum | solution.py:119
  1455.7 32.9 %broadcast_multiply_fusion = f32[64,192,1024]{2,1,0:T(8,128)} fusion(f32[64,192,1024]{2,1,0:T(8,128)} %get-tuple-element.92, f32[64,192]{1,0:T(8,128)S(1)} %rsqrt_multiply_fusion), kind=kLoop, calls=%fused_computation.33 | loop fusion | flops 12582912 | bytes 100712448 | tf_op jit(solution)/shard_map/mul | solution.py:121
  (191 shorter events, 202.8 us)
Async XLA Ops:
  0.6 8.8 copy-start.8
  5.6 73.1 %collective-permute-start = (bf16[64,192,128]{2,1,0:T(8,128)(2,1)}, bf16[64,192,128]{2,1,0:T(8,128)(2,1)}, u32[]{:S(2)}, u32[]{:S(2)}) collective-permute-start(bf16[64,192,128]{2,1,0:T(8,128)(2,1)} %get-tuple-element.99), channel_id=1, source_target_pairs={{0,8},{8,16},{16,24},{24,0},{1,9},{9,17},{17,25},{25,1},{2,10},{10... | collective-permute-start | bytes 9437192 | tf_op jit(solution)/shard_map/ppermute | solution.py:19
  7.2 137.1 %collective-permute-start.1 = (bf16[64,192,128]{2,1,0:T(8,128)(2,1)S(1)}, bf16[64,192,128]{2,1,0:T(8,128)(2,1)}, u32[]{:S(2)}, u32[]{:S(2)}) collective-permute-start(bf16[64,192,128]{2,1,0:T(8,128)(2,1)S(1)} %get-tuple-element.100), channel_id=1, source_target_pairs={{8,0},{16,8},{24,16},{0,24},{9,1},{17,9},{25,17},{1,25},{10,2},{18... | collective-permute-start | bytes 9437192 | tf_op jit(solution)/shard_map/ppermute | solution.py:21
  9.5 0.8 copy-start.12
  9.6 0.9 copy-start.16
  524.8 19.5 %copy-start.18 = (f32[192]{0:T(256)S(1)}, f32[192]{0:T(256)}, u32[]{:S(2)}) copy-start(f32[192]{0:T(256)} %get-tuple-element.77) | copy-start | bytes 2308
  524.8 19.6 %copy-start.19 = (f32[192]{0:T(256)S(1)}, f32[192]{0:T(256)}, u32[]{:S(2)}) copy-start(f32[192]{0:T(256)} %param.9) | copy-start | bytes 2308
  524.8 381.2 %copy-start.13 = (f32[1,192]{1,0:T(1,128)S(1)}, f32[1,192]{1,0:T(1,128)}, u32[]{:S(2)}) copy-start(f32[1,192]{1,0:T(1,128)} %copy-done.12) | copy-start | bytes 2308
  524.8 381.2 %copy-start.17 = (f32[192]{0:T(256)S(1)}, f32[192]{0:T(256)}, u32[]{:S(2)}) copy-start(f32[192]{0:T(256)} %copy-done.16) | copy-start | bytes 2308
  537.6 362.6 %collective-permute-start.2 = (bf16[64,128,1024]{2,1,0:T(8,128)(2,1)S(1)}, bf16[64,128,1024]{2,1,0:T(8,128)(2,1)S(1)}, u32[]{:S(2)}, u32[]{:S(2)}) collective-permute-start(bf16[64,128,1024]{2,1,0:T(8,128)(2,1)S(1)} %get-tuple-element.97), channel_id=1, source_target_pairs={{0,1},{1,2},{2,3},{3,4},{4,5},{5,6},{6,7},{8,9},{9,10},{10,11},{11... | collective-permute-start | bytes 50331656 | tf_op jit(solution)/shard_map/ppermute | solution.py:31
  539.6 361.5 %collective-permute-start.3 = (bf16[64,128,1024]{2,1,0:T(8,128)(2,1)S(1)}, bf16[64,128,1024]{2,1,0:T(8,128)(2,1)}, u32[]{:S(2)}, u32[]{:S(2)}) collective-permute-start(bf16[64,128,1024]{2,1,0:T(8,128)(2,1)S(1)} %get-tuple-element.98), channel_id=1, source_target_pairs={{1,0},{2,1},{3,2},{4,3},{5,4},{6,5},{7,6},{9,8},{10,9},{11,10},{12... | collective-permute-start | bytes 50331656 | tf_op jit(solution)/shard_map/ppermute | solution.py:31
  900.2 5.8 copy-start.20
  944.7 35.1 %copy-start.7 = (f32[192,1024]{1,0:T(8,128)S(1)}, f32[192,1024]{1,0:T(8,128)}, u32[]{:S(2)}) copy-start(f32[192,1024]{1,0:T(8,128)} %param.11) | copy-start | bytes 2359300
  981.0 35.1 %copy-start.5 = (f32[1,192,1024]{2,1,0:T(8,128)}, f32[1,192,1024]{2,1,0:T(8,128)S(1)}, u32[]{:S(2)}) copy-start(f32[1,192,1024]{2,1,0:T(8,128)S(1)} %slice_add_fusion.6) | copy-start | bytes 2359300
  1032.8 12.7 copy-start
  1032.8 12.7 copy-start.9
  1045.5 6.2 copy-start.10
  1045.5 7.1 copy-start.11
  1051.8 2.6 copy-start.3
  1051.8 1.1 copy-start.14
  1059.7 12.5 slice-start.4
  1081.1 18.1 %slice-start.2 = ((s8[6291456]{0:T(1024)(128)(4,1)}), s8[2097152]{0:T(1024)(128)(4,1)S(1)}, s32[]{:S(2)}) async-start(s8[6291456]{0:T(1024)(128)(4,1)} %bitcast.36), calls=%async_computation.2 | async-start | bytes 4194304
  1088.1 11.2 slice-start.3
  1099.2 7.1 slice-start.1
  1099.2 7.1 copy-start.4
  1134.3 18.7 %copy-start.1 = (f32[16,192,1024]{2,1,0:T(8,128)S(1)}, f32[16,192,1024]{2,1,0:T(8,128)}, u32[]{:S(2)}) copy-start(f32[16,192,1024]{2,1,0:T(8,128)} %pad.43) | copy-start | bytes 37748740
  1153.0 11.4 slice-start
  1255.7 31.4 %copy-start.2 = (f32[31,192,1024]{2,1,0:T(8,128)S(1)}, f32[31,192,1024]{2,1,0:T(8,128)}, u32[]{:S(2)}) copy-start(f32[31,192,1024]{2,1,0:T(8,128)} %fusion.28) | copy-start | bytes 73138176
  1255.7 31.6 %copy-start.6 = (f32[1,192,1024]{2,1,0:T(8,128)S(1)}, f32[1,192,1024]{2,1,0:T(8,128)}, u32[]{:S(2)}) copy-start(f32[1,192,1024]{2,1,0:T(8,128)} %copy-done.5) | copy-start | bytes 2359300
  1388.8 66.8 %copy-start.15 = (f32[192]{0:T(256)S(1)}, f32[192]{0:T(256)}, u32[]{:S(2)}) copy-start(f32[192]{0:T(256)} %param.10) | copy-start | bytes 2308
where the time goes:
time: 1490 us
  waiting for transfers between devices  489 us (33%)
  other arithmetic  356 us (24%)
  local copies, waits for them, and re-layouts  320 us (21%)
  matrix products  292 us (20%)
  blocking collectives  18.8 us (1%)
    ppermute x2, waiting for transfers between devices, passed_along(): return lax.ppermute(array, axis, pairs)  356 us
    dot_general x24, matrix products, span_block(): jnp.einsum('yjz,ypj->ypz', matrix, noise_rows, preferred_element_type=jnp...  253 us
    pad x10, local copies, waits for them, and re-layouts, body(): _, states = lax.associative_scan(combine, (factors, driven), axis=0)  183 us
    add x9, other arithmetic, combine(): return (earlier[0] * later[0], later[0] * earlier[1] + later[1])  97.6 us
    ppermute x1, waiting for transfers between devices, extended_2(): lax.ppermute(tail, axis, [(i, (i + 1) % count) for i in range(count)])  68.2 us
    ppermute x1, waiting for transfers between devices, extended_2(): lax.ppermute(head, axis, [((i + 1) % count, i) for i in range(count)])  65.5 us
    add x5, other arithmetic, body(): _, states = lax.associative_scan(combine, (factors, driven), axis=0)  51.1 us
    reduce_sum x1, other arithmetic, body(): energy = lax.psum(jnp.sum(states * states, axis=2), 'span')  48 us
  transfers between devices with their start and end apart: 4, of which 4 were waited for; matrix products, arithmetic and copies ran while one was open for 0% of the time, Pallas kernels for 0%

commit v1 on v0

--- a/solution.py
+++ b/solution.py
@@ -1,12 +1,17 @@
+import functools
 import math
 
 import jax
 import jax.numpy as jnp
 from jax import lax
+from jax.experimental import pallas as pl
+from jax.experimental.pallas import tpu as pltpu
 from jax.sharding import PartitionSpec as P
 
 NZ = 4096
 MAXW = 128
+LANES = 128
+ROWS = 16
 
 
 def extended_2(cells, sides, width):
@@ -63,7 +68,7 @@
     return (earlier[0] * later[0], later[0] * earlier[1] + later[1])
 
 
-def body(random_field, half_widths, time_scale, target_rms, previous_state):
+def plain_body(random_field, half_widths, time_scale, target_rms, previous_state):
     planes, row_count, col_count = random_field.shape
     first_row = lax.axis_index("wall") * row_count
     wall_half = half_widths[0]
@@ -122,7 +127,435 @@
     return (inflow, states[-1])
 
 
+def toeplitz(taps):
+    rolled = pltpu.roll(
+        jnp.broadcast_to(taps, (LANES, 2 * LANES)), 0, 1, stride=1, stride_axis=0
+    )
+    i = lax.broadcasted_iota(jnp.int32, (LANES, LANES), 0)
+    j = lax.broadcasted_iota(jnp.int32, (LANES, LANES), 1)
+    outer = rolled[:, LANES:]
+    parts = [jnp.where(i >= j, outer, 0.0), rolled[:, :LANES], jnp.where(i <= j, outer, 0.0)]
+    return jnp.concatenate([part.astype(jnp.bfloat16) for part in parts], axis=0)
+
+
+def span_kernel(blocks, direct, flag_ref, taps_ref, left_ref, field_ref, right_ref, *refs):
+    head_ref, tail_ref = refs[:2]
+    planes, rows, cols = field_ref.shape
+    tiles = cols // LANES
+    step = pl.program_id(0)
+    extended = jnp.concatenate([left_ref[...], field_ref[...], right_ref[...]], axis=2)
+    by_row = jnp.swapaxes(extended, 0, 1)
+    out = []
+    for row in range(rows):
+        window = jnp.concatenate(
+            [by_row[row, :, t * LANES : (t + 3) * LANES] for t in range(tiles)], axis=0
+        )
+        wide = jnp.dot(
+            window, toeplitz(taps_ref[row : row + 1, :]), preferred_element_type=jnp.float32
+        ).astype(jnp.bfloat16)
+        out.append(
+            jnp.concatenate([wide[t * planes : (t + 1) * planes] for t in range(tiles)], axis=1)
+        )
+    spanned = jnp.swapaxes(jnp.stack(out, axis=0), 0, 1)
+    edge = MAXW // rows
+    in_head = step < edge
+    in_tail = step >= blocks - edge
+
+    @pl.when(in_head)
+    def _():
+        head_ref[...] = spanned
+
+    @pl.when(in_tail)
+    def _():
+        tail_ref[...] = spanned
+
+    if direct < planes:
+        use_head = flag_ref[0] == 1
+
+        @pl.when((use_head & in_head) | (jnp.logical_not(use_head) & in_tail))
+        def _():
+            if direct:
+                refs[2][...] = spanned[:direct]
+            refs[-1][...] = spanned[direct:]
+
+
+def span_filter(flag, taps, left, field, right, first, relayed):
+    planes = left.shape[0]
+    _, row_count, cols = field.shape
+    blocks = row_count // ROWS
+    edge = MAXW // ROWS
+
+    def head(i, flag_ref):
+        return (0, jnp.minimum(i, edge - 1), 0)
+
+    def tail(i, flag_ref):
+        return (0, jnp.maximum(i - (blocks - edge), 0), 0)
+
+    def either(i, flag_ref):
+        low = jnp.minimum(i, edge - 1)
+        high = jnp.maximum(i - (blocks - edge), 0)
+        return (0, jnp.where(flag_ref[0] == 1, low, high), 0)
+
+    direct = planes - relayed
+    outs = [(planes, head), (planes, tail)]
+    if relayed:
+        outs += [(direct, either)] if direct else []
+        outs += [(relayed, either)]
+    side = pl.BlockSpec((planes, ROWS, LANES), lambda i, f: (0, i, 0))
+    return pl.pallas_call(
+        functools.partial(span_kernel, blocks, direct),
+        grid_spec=pltpu.PrefetchScalarGridSpec(
+            num_scalar_prefetch=1,
+            grid=(blocks,),
+            in_specs=[
+                pl.BlockSpec((ROWS, 2 * LANES), lambda i, f: (i, 0)),
+                side,
+                pl.BlockSpec(
+                    (pl.Element(planes), pl.Element(ROWS), pl.Element(cols)),
+                    lambda i, f: (first, i * ROWS, 0),
+                ),
+                side,
+            ],
+            out_specs=[pl.BlockSpec((n, ROWS, cols), m) for n, m in outs],
+        ),
+        out_shape=[jax.ShapeDtypeStruct((n, MAXW, cols), jnp.bfloat16) for n, m in outs],
+        cost_estimate=pl.CostEstimate(
+            flops=2 * planes * row_count * cols * 3 * LANES,
+            bytes_accessed=5 * planes * row_count * cols,
+            transcendentals=0,
+        ),
+        name="span_filter",
+    )(flag, taps, left, field, right)
+
+
+def wall_kernel(
+    group, first, direct, relayed, emit, flag_ref, matrix_ref, decay_ref, gain_ref, start_ref,
+    sums_ref, low_ref, head_ref, tail_ref, high_ref, *refs
+):
+    outs = refs[-4:] if emit else refs[-3:]
+    filtered_ref, state_ref, energy_ref = outs[:3]
+    row_count, cols = state_ref.shape
+    step = pl.program_id(0)
+    rest = row_count - MAXW
+    wide = 2 * LANES
+
+    @pl.when(step == 0)
+    def _():
+        state_ref[...] = start_ref[...]
+        energy_ref[...] = sums_ref[...]
+
+    decay = decay_ref[...]
+    gain = gain_ref[...]
+    above = matrix_ref[:, : 2 * MAXW]
+    below = matrix_ref[:, 2 * MAXW :]
+    lane = lax.broadcasted_iota(jnp.int32, (row_count, LANES), 1)
+    for g in range(group):
+        total = jnp.zeros((row_count, LANES), jnp.float32)
+        for c in range(cols // wide):
+            at = slice(c * wide, (c + 1) * wide)
+            low = low_ref[g, :, at]
+            high = high_ref[g, :, at]
+            if relayed:
+                crossed = refs[0][g, :, at]
+                if direct:
+                    crossed = jnp.where(step * group < direct, crossed, refs[1][g, :, at])
+                low = jnp.where(flag_ref[0] == 1, crossed, low)
+                high = jnp.where(flag_ref[0] == 2, crossed, high)
+            upper = jnp.concatenate([low, head_ref[g, :, at]], axis=0)
+            lower = jnp.concatenate([tail_ref[g, MAXW - rest :, at], high], axis=0)
+            summed = jnp.dot(above, upper, preferred_element_type=jnp.float32) + jnp.dot(
+                below, lower, preferred_element_type=jnp.float32
+            )
+            rounded = summed.astype(jnp.bfloat16)
+            filtered_ref[g, :, at] = rounded
+            driven = rounded.astype(jnp.float32)
+            for h in range(wide // LANES):
+                cell = slice(c * wide + h * LANES, c * wide + (h + 1) * LANES)
+                state = decay * state_ref[:, cell] + gain * driven[:, h * LANES : (h + 1) * LANES]
+                state_ref[:, cell] = state
+                total = total + state * state
+        sums = jnp.sum(total, axis=1, keepdims=True)
+        energy_ref[...] = jnp.where(
+            lane == first + step * group + g, sums, energy_ref[...]
+        )
+    if emit:
+
+        @pl.when(step == pl.num_programs(0) - 1)
+        def _():
+            outs[3][...] = jnp.transpose(energy_ref[...])[emit[0] : emit[1]]
+
+
+def wall_filter(flag, matrix, decay, gain, start, sums, first, rims, crossed, emit):
+    planes, _, cols = rims[1].shape
+    row_count = start.shape[0]
+    relayed = crossed[-1].shape[0] if crossed else 0
+    direct = planes - relayed
+    group = math.gcd(math.gcd(planes, 4), relayed)
+    steps = direct // group
+    rim = pl.BlockSpec((group, MAXW, cols), lambda p, f: (p, 0, 0))
+    whole = lambda a: pl.BlockSpec(a.shape, lambda p, f: (0, 0))
+    energy = jax.ShapeDtypeStruct((row_count, LANES), jnp.float32)
+    extra = []
+    if relayed:
+        if direct:
+            extra.append(
+                pl.BlockSpec(
+                    (group, MAXW, cols), lambda p, f: (jnp.minimum(p, steps - 1), 0, 0)
+                )
+            )
+        extra.append(
+            pl.BlockSpec((group, MAXW, cols), lambda p, f: (jnp.maximum(p - steps, 0), 0, 0))
+        )
+    operands = [matrix, decay, gain, start, sums]
+    outs = [
+        jax.ShapeDtypeStruct((planes, row_count, cols), jnp.bfloat16),
+        jax.ShapeDtypeStruct(start.shape, jnp.float32),
+        energy,
+    ]
+    out_specs = [
+        pl.BlockSpec((group, row_count, cols), lambda p, f: (p, 0, 0)),
+        whole(start),
+        whole(energy),
+    ]
+    if emit:
+        outs.append(jax.ShapeDtypeStruct((emit[1] - emit[0], row_count), jnp.float32))
+        out_specs.append(whole(outs[-1]))
+    return pl.pallas_call(
+        functools.partial(wall_kernel, group, first, direct, relayed, emit),
+        grid_spec=pltpu.PrefetchScalarGridSpec(
+            num_scalar_prefetch=1,
+            grid=(planes // group,),
+            in_specs=[whole(a) for a in operands] + [rim] * 4 + extra,
+            out_specs=out_specs,
+        ),
+        out_shape=outs,
+        cost_estimate=pl.CostEstimate(
+            flops=2 * planes * row_count * cols * matrix.shape[1],
+            bytes_accessed=8 * planes * row_count * cols,
+            transcendentals=0,
+        ),
+        name="wall_filter",
+    )(flag, *operands, *rims, *crossed)
+
+
+def scale_kernel(
+    parts, first, cells, decay_ref, gain_ref, rms_ref, start_ref, filtered_ref, *refs
+):
+    out_ref, scale_ref = refs[-2:]
+    planes, rows, cols = filtered_ref.shape
+    step = pl.program_id(0)
+
+    @pl.when(step == 0)
+    def _():
+        total = refs[0][...]
+        for ref in refs[1:parts]:
+            total = total + ref[...]
+        count, row_count = total.shape
+        total = jnp.concatenate(
+            [total, jnp.zeros((LANES - count, row_count), jnp.float32)], axis=0
+        )
+        scale_ref[...] = rms_ref[...] / jnp.sqrt(jnp.transpose(total) / cells + 1e-06)
+
+    scale = scale_ref[pl.ds(step * rows, rows), :]
+    wide = [
+        jnp.broadcast_to(scale[:, p : p + 1], (rows, LANES))
+        for p in range(first, first + planes)
+    ]
+    decay = decay_ref[...]
+    gain = gain_ref[...]
+    for c in range(cols // LANES):
+        at = slice(c * LANES, (c + 1) * LANES)
+        state = start_ref[:, at]
+        for p in range(planes):
+            state = decay * state + gain * filtered_ref[p, :, at].astype(jnp.float32)
+            out_ref[p, :, at] = state * wide[p]
+
+
+def rescale(decay, gain, rms, start, filtered, energies, offset, target, first, total_planes):
+    planes, row_count, cols = filtered.shape
+    rows = ROWS * math.gcd(row_count // ROWS, 3)
+    narrow = pl.BlockSpec((rows, LANES), lambda i: (i, 0))
+    whole = lambda a: pl.BlockSpec(a.shape, lambda i: (0, 0))
+    operands = [decay, gain, rms, start, filtered, *energies]
+    in_specs = [
+        narrow,
+        narrow,
+        whole(rms),
+        pl.BlockSpec((rows, cols), lambda i: (i, 0)),
+        pl.BlockSpec((planes, rows, cols), lambda i: (0, i, 0)),
+    ] + [whole(e) for e in energies]
+    aliases = {}
+    if target is not None:
+        aliases = {len(operands): 0}
+        operands.append(target)
+        in_specs.append(pl.BlockSpec(memory_space=pl.ANY))
+    return pl.pallas_call(
+        functools.partial(scale_kernel, len(energies), first - offset, float(NZ)),
+        grid=(row_count // rows,),
+        in_specs=in_specs,
+        out_specs=pl.BlockSpec(
+            (pl.Element(planes), pl.Element(rows), pl.Element(cols)),
+            lambda i: (first, i * rows, 0),
+        ),
+        out_shape=jax.ShapeDtypeStruct((total_planes, row_count, cols), jnp.float32),
+        scratch_shapes=[pltpu.VMEM((row_count, LANES), jnp.float32)],
+        input_output_aliases=aliases,
+        cost_estimate=pl.CostEstimate(
+            flops=4 * planes * row_count * cols,
+            bytes_accessed=6 * planes * row_count * cols,
+            transcendentals=0,
+        ),
+        name="rescale",
+    )(*operands)
+
+
+def span_taps(half_width):
+    place = jnp.arange(2 * LANES)
+    offsets = jnp.where(place <= LANES, place, place - 2 * LANES).astype(jnp.float32)
+    values = kernel_values(half_width, kernel_norm(half_width), offsets[None, :])
+    return values.astype(jnp.float32)
+
+
+def neighbour_pairs(count, by, skip=()):
+    return [
+        (i, i + by) for i in range(count) if 0 <= i + by < count and (i, i + by) not in skip
+    ]
+
+
+CHUNKS = (8, 12, 16, 16, 12)
+RELAYED = (0, 12, 12, 8, 0)
+SUMMED = (1, 2, 3, 4)
+ORDER = (
+    "H0 H1 S0 U0",
+    "D0 H2 S1 H3",
+    "V1 U1 D1 S2",
+    "V2 U2 D2 Q2",
+    "X1 H4 S3 V3",
+    "U3 D3 Q3 W0",
+    "S4 X2 U4 D4",
+    "X3 W1 E1 F0",
+    "F1 W2 E2 F2",
+    "W3 E3 F3 W4",
+    "E4 F4",
+)
+
+
+def relay_plan(walls):
+    return RELAYED if walls == 8 else (0,) * len(CHUNKS)
+
+
+def sequence(relayed, spans):
+    names = []
+    for item in " ".join(ORDER).split():
+        kind, c = item[0], int(item[1:])
+        if kind == "H":
+            names += [item + "l", item + "r"]
+        elif kind == "E":
+            names += [f"{item}s{s}" for s in range(1, spans)]
+        elif kind in "VX":
+            names += [item] if relayed[c] else []
+        elif kind == "Q":
+            names += [item] if 0 < relayed[c] < CHUNKS[c] else []
+        else:
+            names.append(item)
+    return names
+
+
+def body(random_field, half_widths, time_scale, target_rms, previous_state):
+    planes, row_count, cols = random_field.shape
+    spans = lax.axis_size("span")
+    walls = lax.axis_size("wall")
+    here = lax.axis_index("wall")
+    first_row = here * row_count
+    middle = walls // 2
+    relayed = relay_plan(walls)
+    firsts = [sum(CHUNKS[:c]) for c in range(len(CHUNKS))]
+
+    span_local = lax.dynamic_slice_in_dim(half_widths[1], first_row, row_count)
+    taps = span_taps(span_local)
+    matrix = wall_matrix(half_widths[0], first_row, row_count)
+    spread = lambda v: jnp.broadcast_to(v[:, None], (row_count, LANES))
+    decay = spread(jnp.exp(-math.pi / (2.0 * time_scale)))
+    gain = spread(jnp.sqrt(1.0 - jnp.exp(-math.pi / time_scale)))
+    rms = spread(target_rms)
+    flag = jnp.where(here == middle, 1, jnp.where(here == middle - 1, 2, 0)).astype(jnp.int32)
+    flag = flag.reshape(1)
+
+    crossing = ((middle - 1, middle), (middle, middle - 1))
+    made = {}
+    states = [previous_state]
+    sums = jnp.zeros((row_count, LANES), jnp.float32)
+    target = None
+    for name in sequence(relayed, spans):
+        kind, c = name[0], int(name[1:2])
+        first, size = firsts[c], CHUNKS[c]
+        skip = crossing if relayed[c] else ()
+        if kind == "H":
+            part = lax.slice_in_dim(random_field, first, first + size, axis=0)
+            if name.endswith("l"):
+                edge = part[:, :, cols - MAXW :]
+                pairs = [(i, (i + 1) % spans) for i in range(spans)]
+            else:
+                edge = part[:, :, :MAXW]
+                pairs = [((i + 1) % spans, i) for i in range(spans)]
+            made[name] = lax.ppermute(edge, "span", pairs)
+        elif kind == "S":
+            left, right = made[f"H{c}l"], made[f"H{c}r"]
+            made[name] = span_filter(
+                flag, taps, left, random_field, right, first, relayed[c]
+            )
+        elif kind == "U":
+            tail = made[f"S{c}"][1]
+            made[name] = lax.ppermute(tail, "wall", neighbour_pairs(walls, 1, skip))
+        elif kind == "D":
+            head = made[f"S{c}"][0]
+            made[name] = lax.ppermute(head, "wall", neighbour_pairs(walls, -1, skip))
+        elif kind == "Q":
+            made[name] = lax.ppermute(made[f"S{c}"][2], "wall", crossing)
+        elif kind == "V":
+            out = [(middle - 1, walls - 1), (middle, 0)]
+            made[name] = lax.ppermute(made[f"S{c}"][-1], "wall", out)
+        elif kind == "X":
+            back = [(walls - 1, middle), (0, middle - 1)]
+            made[name] = lax.ppermute(made[f"V{c}"], "wall", back)
+        elif kind == "W":
+            head, tail = made[f"S{c}"][:2]
+            rims = (made[f"U{c}"], head, tail, made[f"D{c}"])
+            crossed = [made[k] for k in (f"Q{c}", f"X{c}") if k in made]
+            emit = None
+            if c in SUMMED:
+                start = max([firsts[e + 1] for e in SUMMED if e < c], default=0)
+                emit = (start // 8 * 8, -(-(first + size) // 8) * 8)
+            made[name], state, sums, *out = wall_filter(
+                flag, matrix, decay, gain, states[c], sums, first, rims, crossed, emit
+            )
+            states.append(state)
+            if emit:
+                made[f"E{c}"] = (emit[0], out)
+        elif kind == "E":
+            by = int(name.split("s")[1])
+            pairs = [(i, (i + by) % spans) for i in range(spans)]
+            energies = made[f"E{c}"][1]
+            energies.append(lax.ppermute(energies[0], "span", pairs))
+        else:
+            offset, energies = made[f"E{min(e for e in SUMMED if e >= c)}"]
+            filtered = made[f"W{c}"]
+            target = rescale(
+                decay, gain, rms, states[c], filtered, energies, offset, target, first, planes
+            )
+    return (target, states[-1])
+
+
 def solution(mesh):
     in_specs = (P(None, "wall", "span"), P(), P("wall"), P("wall"), P("wall", "span"))
     out_specs = (P(None, "wall", "span"), P("wall", "span"))
-    return jax.shard_map(body, mesh=mesh, in_specs=in_specs, out_specs=out_specs, check_vma=False)
+
+    def step(random_field, *rest):
+        planes, row_count, cols = random_field.shape
+        fits = MAXW <= row_count <= 2 * MAXW and row_count % ROWS == 0
+        fits = fits and planes == sum(CHUNKS) and cols % (2 * LANES) == 0
+        return (body if fits else plain_body)(random_field, *rest)
+
+    return jax.shard_map(
+        step, mesh=mesh, in_specs=in_specs, out_specs=out_specs, check_vma=False
+    )

time: 1490 us -> 513 us (0.34)
  the two profiles are of different devices: /device:TPU:4 before, /device:TPU:6 now
where the time goes in v1:
time: 513 us; the launch traced here: 511 us
  Pallas kernels  168 us (33%)
  starting transfers between devices  161 us (31%)
  waiting for transfers between devices  160 us (31%)
  local copies, waits for them, and re-layouts  16.7 us (3%)
    ppermute x5, waiting for transfers between devices, body(): made[name] = lax.ppermute(head, 'wall', neighbour_pairs(walls, -1, skip))  83.2 us
    pallas_call x5, Pallas kernels, span_filter(): pl.pallas_call(functools.partial(span_kernel, blocks, direct), grid_spec=...  74.2 us
    ppermute x5, starting transfers between devices, body(): made[name] = lax.ppermute(head, 'wall', neighbour_pairs(walls, -1, skip))  71.4 us
    ppermute x5, waiting for transfers between devices, body(): made[name] = lax.ppermute(tail, 'wall', neighbour_pairs(walls, 1, skip))  66.7 us
    pallas_call x5, Pallas kernels, wall_filter(): pl.pallas_call(functools.partial(wall_kernel, group, first, direct, relay...  55.6 us
    ppermute x10, starting transfers between devices, body(): made[name] = lax.ppermute(edge, 'span', pairs)  47.2 us
    pallas_call x5, Pallas kernels, rescale(): pl.pallas_call(functools.partial(scale_kernel, len(energies), first - off...  38.3 us
    ppermute x12, starting transfers between devices, body(): energies.append(lax.ppermute(energies[0], 'span', pairs))  17.7 us
  transfers between devices with their start and end apart: 40, of which 7 were waited for; matrix products, arithmetic and copies ran while one was open for 3% of the time, Pallas kernels for 31%

profile of v1, /device:TPU:6, one launch (start us, length us, event | category | flops | bytes accessed | tf_op | source)
XLA Modules:
  0.0 510.5 jit_solution(6880386129030484987)
XLA Ops:
  3.4 2.2 collective-permute-start.1
  5.7 3.0 fusion.15
  8.7 3.8 collective-permute-start.5
  12.5 3.7 fusion.16
  17.0 9.6 %collective-permute-start.11 = (bf16[16,192,128]{2,1,0:T(8,128)(2,1)}, bf16[16,192,128]{2,1,0:T(8,128)(2,1)S(1)}, u32[]{:S(2)}, u32[]{:S(2)}) collective-permute-start(bf16[16,192,128]{2,1,0:T(8,128)(2,1)} %get-tuple-element.76), channel_id=1, source_target_pairs={{8,0},{16,8},{24,16},{0,24},{9,1},{17,9},{25,17},{1,25},{10,2},{18... | collective-permute-start | bytes 2359304 | tf_op jit(solution)/shard_map/ppermute | solution.py:501
  28.0 8.8 %collective-permute-done.4.left_ref = bf16[12,192,128]{2,1,0:T(8,128)(2,1)S(1)} collective-permute-done((bf16[12,192,128]{2,1,0:T(8,128)(2,1)S(1)}, bf16[12,192,128]{2,1,0:T(8,128)(2,1)S(1)}, u32[]{:S(2)}, u32[]{:S(2)}) %collective-permute-start.4) | collective-permute-done | bytes 589856 | tf_op jit(solution)/shard_map/ppermute | solution.py:501
  37.7 14.4 %collective-permute-start.18 = (bf16[16,192,128]{2,1,0:T(8,128)(2,1)}, bf16[16,192,128]{2,1,0:T(8,128)(2,1)S(1)}, u32[]{:S(2)}, u32[]{:S(2)}) collective-permute-start(bf16[16,192,128]{2,1,0:T(8,128)(2,1)} %get-tuple-element.74), channel_id=1, source_target_pairs={{8,0},{16,8},{24,16},{0,24},{9,1},{17,9},{25,17},{1,25},{10,2},{18... | collective-permute-start | bytes 2359304 | tf_op jit(solution)/shard_map/ppermute | solution.py:501
  53.4 12.4 %span_filter.5 = (bf16[8,128,1024]{2,1,0:T(8,128)(2,1)}, bf16[8,128,1024]{2,1,0:T(8,128)(2,1)}) custom-call(s32[1]{0:T(128)} %bitcast.flag_ref, f32[192,256]{1,0:T(8,128)} %fusion.12.taps_ref, bf16[8,192,128]{2,1,0:T(8,128)(2,1)} %copy-done.10, bf16[64,192,1024]{2,1,0:T(8,128)(2,1)} %field_ref.9, bf16[8,192,128]{2,1,0:T(8,128)(2,1)} %collective-permute-done.1.right_ref), custom_call_target="tpu_custom_call" | custom-call | flops 1207959552 | bytes 7864320 | tf_op jit(solution)/shard_map/span_filter/pallas_call | solution.py:205
  65.9 1.9 collective-permute-start.2
  67.8 13.7 %collective-permute-start.24 = (bf16[12,192,128]{2,1,0:T(8,128)(2,1)}, bf16[12,192,128]{2,1,0:T(8,128)(2,1)}, u32[]{:S(2)}, u32[]{:S(2)}) collective-permute-start(bf16[12,192,128]{2,1,0:T(8,128)(2,1)} %get-tuple-element.71), channel_id=1, source_target_pairs={{0,8},{8,16},{16,24},{24,0},{1,9},{9,17},{17,25},{25,1},{2,10},{10... | collective-permute-start | bytes 1769480 | tf_op jit(solution)/shard_map/ppermute | solution.py:501
  83.1 1.8 collective-permute-start.25
  84.9 15.3 %span_filter.6 = (bf16[12,128,1024]{2,1,0:T(8,128)(2,1)}, bf16[12,128,1024]{2,1,0:T(8,128)(2,1)}, bf16[12,128,1024]{2,1,0:T(8,128)(2,1)}) custom-call(s32[1]{0:T(128)} %bitcast.flag_ref, f32[192,256]{1,0:T(8,128)} %fusion.12.taps_ref, bf16[12,192,128]{2,1,0:T(8,128)(2,1)} %copy-done.9, bf16[64,192,1024]{2,1,0:T(8,128)(2,1)} %field_ref.9, ...), custom_call_target="tpu_custom_call" | custom-call | flops 1811939328 | bytes 11796480 | tf_op jit(solution)/shard_map/span_filter/pallas_call | solution.py:205
  100.3 15.9 %span_filter.7 = (bf16[16,128,1024]{2,1,0:T(8,128)(2,1)}, bf16[16,128,1024]{2,1,0:T(8,128)(2,1)}, bf16[4,128,1024]{2,1,0:T(8,128)(2,1)}, bf16[12,128,1024]{2,1,0:T(8,128)(2,1)}) custom-call(s32[1]{0:T(128)} %bitcast.flag_ref, f32[192,256]{1,0:T(8,128)} %fusion.12.taps_ref, bf16[16,192,128]{2,1,0:T(8,128)(2,1)} %copy-done.5, ...), custom_call_target="tpu_custom_call" | custom-call | flops 2415919104 | bytes 15728640 | tf_op jit(solution)/shard_map/span_filter/pallas_call | solution.py:205
  116.2 1.9 collective-permute-start.6
  120.8 15.9 %span_filter.8 = (bf16[16,128,1024]{2,1,0:T(8,128)(2,1)}, bf16[16,128,1024]{2,1,0:T(8,128)(2,1)}, bf16[8,128,1024]{2,1,0:T(8,128)(2,1)}, bf16[8,128,1024]{2,1,0:T(8,128)(2,1)}) custom-call(s32[1]{0:T(128)} %bitcast.flag_ref, f32[192,256]{1,0:T(8,128)} %fusion.12.taps_ref, bf16[16,192,128]{2,1,0:T(8,128)(2,1)} %copy-done.7, bf16[64,192,1024]{2,1,0:T(8,128)(2,1)} %field_ref.9, ...), custom_call_target="tpu_custom_call" | custom-call | flops 2415919104 | bytes 15728640 | tf_op jit(solution)/shard_map/span_filter/pallas_call | solution.py:205
  136.7 3.6 collective-permute-start.3
  142.1 2.4 collective-permute-start.8
  144.5 19.7 %collective-permute-done.3.high_ref = bf16[8,128,1024]{2,1,0:T(8,128)(2,1)S(1)} collective-permute-done((bf16[8,128,1024]{2,1,0:T(8,128)(2,1)}, bf16[8,128,1024]{2,1,0:T(8,128)(2,1)S(1)}, u32[]{:S(2)}, u32[]{:S(2)}) %collective-permute-start.3) | collective-permute-done | bytes 2097184 | tf_op jit(solution)/shard_map/ppermute | solution.py:512
  164.2 1.9 collective-permute-start.12
  166.2 2.3 collective-permute-start.15
  168.5 4.0 collective-permute-start.13
  172.5 12.9 %collective-permute-done.6.low_ref = bf16[12,128,1024]{2,1,0:T(8,128)(2,1)} collective-permute-done((bf16[12,128,1024]{2,1,0:T(8,128)(2,1)}, bf16[12,128,1024]{2,1,0:T(8,128)(2,1)}, u32[]{:S(2)}, u32[]{:S(2)}) %collective-permute-start.6) | collective-permute-done | bytes 3145760 | tf_op jit(solution)/shard_map/ppermute | solution.py:509
  185.4 55.4 %collective-permute-start.7 = (bf16[12,128,1024]{2,1,0:T(8,128)(2,1)S(1)}, bf16[12,128,1024]{2,1,0:T(8,128)(2,1)S(1)}, u32[]{:S(2)}, u32[]{:S(2)}) collective-permute-start(bf16[12,128,1024]{2,1,0:T(8,128)(2,1)S(1)} %copy-done), channel_id=1, source_target_pairs={{1,0},{2,1},{3,2},{5,4},{6,5},{7,6},{9,8},{10,9},{11,10},{13,12},{... | collective-permute-start | bytes 9437192 | tf_op jit(solution)/shard_map/ppermute | solution.py:512
  240.7 2.3 collective-permute-start.9
  243.1 2.4 collective-permute-start.16
  245.5 63.5 %collective-permute-done.7.high_ref = bf16[12,128,1024]{2,1,0:T(8,128)(2,1)S(1)} collective-permute-done((bf16[12,128,1024]{2,1,0:T(8,128)(2,1)S(1)}, bf16[12,128,1024]{2,1,0:T(8,128)(2,1)S(1)}, u32[]{:S(2)}, u32[]{:S(2)}) %collective-permute-start.7) | collective-permute-done | bytes 3145760 | tf_op jit(solution)/shard_map/ppermute | solution.py:512
  309.0 1.8 copy-done.1
  310.8 1.9 collective-permute-start.19
  312.7 4.2 collective-permute-start.20
  316.9 14.6 %span_filter.9 = (bf16[12,128,1024]{2,1,0:T(8,128)(2,1)}, bf16[12,128,1024]{2,1,0:T(8,128)(2,1)}) custom-call(s32[1]{0:T(128)} %bitcast.flag_ref, f32[192,256]{1,0:T(8,128)} %fusion.12.taps_ref, bf16[12,192,128]{2,1,0:T(8,128)(2,1)} %collective-permute-done.24.left_ref, bf16[64,192,1024]{2,1,0:T(8,128)(2,1)} %field_ref.9, ...), custom_call_target="tpu_custom_call" | custom-call | flops 1811939328 | bytes 11796480 | tf_op jit(solution)/shard_map/span_filter/pallas_call | solution.py:205
  331.6 2.1 collective-permute-start.26
  333.7 4.2 collective-permute-start.27
  337.9 2.0 collective-permute-start.23
  342.9 6.9 %wall_filter.5 = (bf16[8,192,1024]{2,1,0:T(8,128)(2,1)}, f32[192,1024]{1,0:T(8,128)}, f32[192,128]{1,0:T(8,128)}) custom-call(s32[1]{0:T(128)} %bitcast.flag_ref, bf16[192,448]{1,0:T(8,128)(2,1)} %fusion.4.matrix_ref, f32[192,128]{1,0:T(8,128)} %broadcast_in_dim.21.decay_ref, f32[192,128]{1,0:T(8,128)} %broadcast_in_dim.22.gain_ref, f32[192,1024]{1,0:T(8,128)} %start_ref.3, ...), custom_call_target="tpu_custom_call" | custom-call | flops 1409286144 | bytes 12582912 | tf_op jit(solution)/shard_map/wall_filter/pallas_call | solution.py:323
  349.8 11.4 %wall_filter.6 = (bf16[12,192,1024]{2,1,0:T(8,128)(2,1)}, f32[192,1024]{1,0:T(8,128)}, f32[192,128]{1,0:T(8,128)}, f32[24,192]{1,0:T(8,128)}) custom-call(s32[1]{0:T(128)} %bitcast.flag_ref, bf16[192,448]{1,0:T(8,128)(2,1)} %fusion.4.matrix_ref, f32[192,128]{1,0:T(8,128)} %broadcast_in_dim.21.decay_ref, f32[192,128]{1,0:T(8,128)} %broadcast_in_dim.22.gain_ref, ...), custom_call_target="tpu_custom_call" | custom-call | flops 2113929216 | bytes 18874368 | tf_op jit(solution)/shard_map/wall_filter/pallas_call | solution.py:323
  361.3 13.7 %wall_filter.7 = (bf16[16,192,1024]{2,1,0:T(8,128)(2,1)}, f32[192,1024]{1,0:T(8,128)}, f32[192,128]{1,0:T(8,128)}, f32[24,192]{1,0:T(8,128)}) custom-call(s32[1]{0:T(128)} %bitcast.flag_ref, bf16[192,448]{1,0:T(8,128)(2,1)} %fusion.4.matrix_ref, f32[192,128]{1,0:T(8,128)} %broadcast_in_dim.21.decay_ref, f32[192,128]{1,0:T(8,128)} %broadcast_in_dim.22.gain_ref, ...), custom_call_target="tpu_custom_call" | custom-call | flops 2818572288 | bytes 25165824 | tf_op jit(solution)/shard_map/wall_filter/pallas_call | solution.py:323
  374.9 53.8 %collective-permute-done.26.low_ref = bf16[12,128,1024]{2,1,0:T(8,128)(2,1)S(1)} collective-permute-done((bf16[12,128,1024]{2,1,0:T(8,128)(2,1)}, bf16[12,128,1024]{2,1,0:T(8,128)(2,1)S(1)}, u32[]{:S(2)}, u32[]{:S(2)}) %collective-permute-start.26) | collective-permute-done | bytes 3145760 | tf_op jit(solution)/shard_map/ppermute | solution.py:509
  429.0 2.4 collective-permute-start.38
  433.4 13.3 %wall_filter.8 = (bf16[16,192,1024]{2,1,0:T(8,128)(2,1)}, f32[192,1024]{1,0:T(8,128)}, f32[192,128]{1,0:T(8,128)}, f32[24,192]{1,0:T(8,128)}) custom-call(s32[1]{0:T(128)} %bitcast.flag_ref, bf16[192,448]{1,0:T(8,128)(2,1)} %fusion.4.matrix_ref, f32[192,128]{1,0:T(8,128)} %broadcast_in_dim.21.decay_ref, f32[192,128]{1,0:T(8,128)} %broadcast_in_dim.22.gain_ref, ...), custom_call_target="tpu_custom_call" | custom-call | flops 2818572288 | bytes 25165824 | tf_op jit(solution)/shard_map/wall_filter/pallas_call | solution.py:323
  448.0 2.9 collective-permute-start.36
  452.0 2.8 collective-permute-start.33
  454.9 10.4 %wall_filter.9 = (bf16[12,192,1024]{2,1,0:T(8,128)(2,1)}, f32[192,1024]{1,0:T(8,128)}, f32[192,128]{1,0:T(8,128)}, f32[16,192]{1,0:T(8,128)}) custom-call(s32[1]{0:T(128)} %bitcast.flag_ref, bf16[192,448]{1,0:T(8,128)(2,1)} %fusion.4.matrix_ref, f32[192,128]{1,0:T(8,128)} %broadcast_in_dim.21.decay_ref, f32[192,128]{1,0:T(8,128)} %broadcast_in_dim.22.gain_ref, ...), custom_call_target="tpu_custom_call" | custom-call | flops 2113929216 | bytes 18874368 | tf_op jit(solution)/shard_map/wall_filter/pallas_call | solution.py:323
  467.4 2.8 collective-permute-start.30
  470.9 5.9 %rescale.5.refs_4_ = f32[64,192,1024]{2,1,0:T(8,128)} custom-call(f32[192,128]{1,0:T(8,128)} %broadcast_in_dim.21.decay_ref, f32[192,128]{1,0:T(8,128)} %broadcast_in_dim.22.gain_ref, f32[192,128]{1,0:T(8,128)} %broadcast_in_dim.23.rms_ref, f32[192,1024]{1,0:T(8,128)} %start_ref.3, bf16[8,192,1024]{2,1,0:T(8,128)(2,1)} %get-tuple-element.66.filtered_ref, ...), custom_call_target="tpu_custom_call" | custom-call | flops 6291456 | bytes 9437184 | tf_op jit(solution)/shard_map/rescale/pallas_call | solution.py:392
  476.9 7.4 %rescale.6.refs_4_ = f32[64,192,1024]{2,1,0:T(8,128)} custom-call(f32[192,128]{1,0:T(8,128)} %broadcast_in_dim.21.decay_ref, f32[192,128]{1,0:T(8,128)} %broadcast_in_dim.22.gain_ref, f32[192,128]{1,0:T(8,128)} %broadcast_in_dim.23.rms_ref, f32[192,1024]{1,0:T(8,128)} %get-tuple-element.37.start_ref, ...), custom_call_target="tpu_custom_call", output_to_operand_aliasing={{}: (9, {})} | custom-call | flops 9437184 | bytes 14155776 | tf_op jit(solution)/shard_map/rescale/pallas_call | solution.py:392
  484.3 8.8 %rescale.7.refs_4_ = f32[64,192,1024]{2,1,0:T(8,128)} custom-call(f32[192,128]{1,0:T(8,128)} %broadcast_in_dim.21.decay_ref, f32[192,128]{1,0:T(8,128)} %broadcast_in_dim.22.gain_ref, f32[192,128]{1,0:T(8,128)} %broadcast_in_dim.23.rms_ref, f32[192,1024]{1,0:T(8,128)} %get-tuple-element.42.start_ref, ...), custom_call_target="tpu_custom_call", output_to_operand_aliasing={{}: (9, {})} | custom-call | flops 12582912 | bytes 18874368 | tf_op jit(solution)/shard_map/rescale/pallas_call | solution.py:392
  493.7 8.8 %rescale.8.refs_4_ = f32[64,192,1024]{2,1,0:T(8,128)} custom-call(f32[192,128]{1,0:T(8,128)} %broadcast_in_dim.21.decay_ref, f32[192,128]{1,0:T(8,128)} %broadcast_in_dim.22.gain_ref, f32[192,128]{1,0:T(8,128)} %broadcast_in_dim.23.rms_ref, f32[192,1024]{1,0:T(8,128)} %get-tuple-element.48.start_ref, ...), custom_call_target="tpu_custom_call", output_to_operand_aliasing={{}: (9, {})} | custom-call | flops 12582912 | bytes 18874368 | tf_op jit(solution)/shard_map/rescale/pallas_call | solution.py:392
  503.2 7.4 %rescale.9 = f32[64,192,1024]{2,1,0:T(8,128)} custom-call(f32[192,128]{1,0:T(8,128)} %broadcast_in_dim.21.decay_ref, f32[192,128]{1,0:T(8,128)} %broadcast_in_dim.22.gain_ref, f32[192,128]{1,0:T(8,128)} %broadcast_in_dim.23.rms_ref, f32[192,1024]{1,0:T(8,128)} %get-tuple-element.54.start_ref, ...), custom_call_target="tpu_custom_call", output_to_operand_aliasing={{}: (9, {})} | custom-call | flops 9437184 | bytes 14155776 | tf_op jit(solution)/shard_map/rescale/pallas_call | solution.py:392
  (126 shorter events, 25.1 us)
Async XLA Ops:
  1.8 14.5 %collective-permute-start = (bf16[8,192,128]{2,1,0:T(8,128)(2,1)S(1)}, bf16[8,192,128]{2,1,0:T(8,128)(2,1)S(1)}, u32[]{:S(2)}, u32[]{:S(2)}) collective-permute-start(bf16[8,192,128]{2,1,0:T(8,128)(2,1)S(1)} %get-tuple-element.79), channel_id=1, source_target_pairs={{0,8},{8,16},{16,24},{24,0},{1,9},{9,17},{17,25},{25,1},{2,10},{10... | collective-permute-start | bytes 1179656 | tf_op jit(solution)/shard_map/ppermute | solution.py:501
  3.4 24.5 %collective-permute-start.1 = (bf16[8,192,128]{2,1,0:T(8,128)(2,1)S(1)}, bf16[8,192,128]{2,1,0:T(8,128)(2,1)}, u32[]{:S(2)}, u32[]{:S(2)}) collective-permute-start(bf16[8,192,128]{2,1,0:T(8,128)(2,1)S(1)} %get-tuple-element.78), channel_id=1, source_target_pairs={{8,0},{16,8},{24,16},{0,24},{9,1},{17,9},{25,17},{1,25},{10,2},{18... | collective-permute-start | bytes 1179656 | tf_op jit(solution)/shard_map/ppermute | solution.py:501
  8.7 28.2 %collective-permute-start.4 = (bf16[12,192,128]{2,1,0:T(8,128)(2,1)S(1)}, bf16[12,192,128]{2,1,0:T(8,128)(2,1)S(1)}, u32[]{:S(2)}, u32[]{:S(2)}) collective-permute-start(bf16[12,192,128]{2,1,0:T(8,128)(2,1)S(1)} %get-tuple-element.73), channel_id=1, source_target_pairs={{0,8},{8,16},{16,24},{24,0},{1,9},{9,17},{17,25},{25,1},{2,10},{10... | collective-permute-start | bytes 1769480 | tf_op jit(solution)/shard_map/ppermute | solution.py:501
  8.7 57.2 %collective-permute-start.5 = (bf16[12,192,128]{2,1,0:T(8,128)(2,1)}, bf16[12,192,128]{2,1,0:T(8,128)(2,1)}, u32[]{:S(2)}, u32[]{:S(2)}) collective-permute-start(bf16[12,192,128]{2,1,0:T(8,128)(2,1)} %get-tuple-element.72), channel_id=1, source_target_pairs={{8,0},{16,8},{24,16},{0,24},{9,1},{17,9},{25,17},{1,25},{10,2},{18... | collective-permute-start | bytes 1769480 | tf_op jit(solution)/shard_map/ppermute | solution.py:501
  16.1 51.7 %collective-permute-start.10 = (bf16[16,192,128]{2,1,0:T(8,128)(2,1)}, bf16[16,192,128]{2,1,0:T(8,128)(2,1)S(1)}, u32[]{:S(2)}, u32[]{:S(2)}) collective-permute-start(bf16[16,192,128]{2,1,0:T(8,128)(2,1)} %get-tuple-element.77), channel_id=1, source_target_pairs={{0,8},{8,16},{16,24},{24,0},{1,9},{9,17},{17,25},{25,1},{2,10},{10... | collective-permute-start | bytes 2359304 | tf_op jit(solution)/shard_map/ppermute | solution.py:501
  17.0 66.1 %collective-permute-start.11 = (bf16[16,192,128]{2,1,0:T(8,128)(2,1)}, bf16[16,192,128]{2,1,0:T(8,128)(2,1)S(1)}, u32[]{:S(2)}, u32[]{:S(2)}) collective-permute-start(bf16[16,192,128]{2,1,0:T(8,128)(2,1)} %get-tuple-element.76), channel_id=1, source_target_pairs={{8,0},{16,8},{24,16},{0,24},{9,1},{17,9},{25,17},{1,25},{10,2},{18... | collective-permute-start | bytes 2359304 | tf_op jit(solution)/shard_map/ppermute | solution.py:501
  28.0 88.2 %collective-permute-start.17 = (bf16[16,192,128]{2,1,0:T(8,128)(2,1)}, bf16[16,192,128]{2,1,0:T(8,128)(2,1)S(1)}, u32[]{:S(2)}, u32[]{:S(2)}) collective-permute-start(bf16[16,192,128]{2,1,0:T(8,128)(2,1)} %get-tuple-element.75), channel_id=1, source_target_pairs={{0,8},{8,16},{16,24},{24,0},{1,9},{9,17},{17,25},{25,1},{2,10},{10... | collective-permute-start | bytes 2359304 | tf_op jit(solution)/shard_map/ppermute | solution.py:501
  37.7 80.5 %collective-permute-start.18 = (bf16[16,192,128]{2,1,0:T(8,128)(2,1)}, bf16[16,192,128]{2,1,0:T(8,128)(2,1)S(1)}, u32[]{:S(2)}, u32[]{:S(2)}) collective-permute-start(bf16[16,192,128]{2,1,0:T(8,128)(2,1)} %get-tuple-element.74), channel_id=1, source_target_pairs={{8,0},{16,8},{24,16},{0,24},{9,1},{17,9},{25,17},{1,25},{10,2},{18... | collective-permute-start | bytes 2359304 | tf_op jit(solution)/shard_map/ppermute | solution.py:501
  65.9 76.3 %collective-permute-start.2 = (bf16[8,128,1024]{2,1,0:T(8,128)(2,1)}, bf16[8,128,1024]{2,1,0:T(8,128)(2,1)}, u32[]{:S(2)}, u32[]{:S(2)}) collective-permute-start(bf16[8,128,1024]{2,1,0:T(8,128)(2,1)} %get-tuple-element.35.tail_ref), channel_id=1, source_target_pairs={{0,1},{1,2},{2,3},{3,4},{4,5},{5,6},{6,7},{8,9},{9,10},{10,11},{11... | collective-permute-start | bytes 6291464 | tf_op jit(solution)/shard_map/ppermute | solution.py:509
  67.8 32.5 %copy-start.5 = (bf16[16,192,128]{2,1,0:T(8,128)(2,1)}, bf16[16,192,128]{2,1,0:T(8,128)(2,1)S(1)}, u32[]{:S(2)}) copy-start(bf16[16,192,128]{2,1,0:T(8,128)(2,1)S(1)} %collective-permute-done.10.left_ref) | copy-start | bytes 2359300
  67.8 68.9 %collective-permute-start.24 = (bf16[12,192,128]{2,1,0:T(8,128)(2,1)}, bf16[12,192,128]{2,1,0:T(8,128)(2,1)}, u32[]{:S(2)}, u32[]{:S(2)}) collective-permute-start(bf16[12,192,128]{2,1,0:T(8,128)(2,1)} %get-tuple-element.71), channel_id=1, source_target_pairs={{0,8},{8,16},{16,24},{24,0},{1,9},{9,17},{17,25},{25,1},{2,10},{10... | collective-permute-start | bytes 1769480 | tf_op jit(solution)/shard_map/ppermute | solution.py:501
  83.1 57.4 %collective-permute-start.25 = (bf16[12,192,128]{2,1,0:T(8,128)(2,1)}, bf16[12,192,128]{2,1,0:T(8,128)(2,1)}, u32[]{:S(2)}, u32[]{:S(2)}) collective-permute-start(bf16[12,192,128]{2,1,0:T(8,128)(2,1)} %get-tuple-element.70), channel_id=1, source_target_pairs={{8,0},{16,8},{24,16},{0,24},{9,1},{17,9},{25,17},{1,25},{10,2},{18... | collective-permute-start | bytes 1769480 | tf_op jit(solution)/shard_map/ppermute | solution.py:501
  116.2 69.2 %collective-permute-start.6 = (bf16[12,128,1024]{2,1,0:T(8,128)(2,1)}, bf16[12,128,1024]{2,1,0:T(8,128)(2,1)}, u32[]{:S(2)}, u32[]{:S(2)}) collective-permute-start(bf16[12,128,1024]{2,1,0:T(8,128)(2,1)} %get-tuple-element.39.tail_ref), channel_id=1, source_target_pairs={{0,1},{1,2},{2,3},{4,5},{5,6},{6,7},{8,9},{9,10},{10,11},{12,13},{... | collective-permute-start | bytes 9437192 | tf_op jit(solution)/shard_map/ppermute | solution.py:509
  119.0 66.3 %copy-start = (bf16[12,128,1024]{2,1,0:T(8,128)(2,1)S(1)}, bf16[12,128,1024]{2,1,0:T(8,128)(2,1)}, u32[]{:S(2)}) copy-start(bf16[12,128,1024]{2,1,0:T(8,128)(2,1)} %get-tuple-element.40.head_ref) | copy-start | bytes 9437188
  119.0 22.3 %collective-permute-start.14 = (bf16[4,128,1024]{2,1,0:T(8,128)(2,1)}, bf16[4,128,1024]{2,1,0:T(8,128)(2,1)}, u32[]{:S(2)}, u32[]{:S(2)}) collective-permute-start(bf16[4,128,1024]{2,1,0:T(8,128)(2,1)} %get-tuple-element.46), channel_id=1, source_target_pairs={{3,4},{4,3},{11,12},{12,11},{19,20},{20,19},{27,28},{28,27}} | collective-permute-start | bytes 3145736 | tf_op jit(solution)/shard_map/ppermute | solution.py:514
  136.7 27.5 %collective-permute-start.3 = (bf16[8,128,1024]{2,1,0:T(8,128)(2,1)}, bf16[8,128,1024]{2,1,0:T(8,128)(2,1)S(1)}, u32[]{:S(2)}, u32[]{:S(2)}) collective-permute-start(bf16[8,128,1024]{2,1,0:T(8,128)(2,1)} %get-tuple-element.36.head_ref), channel_id=1, source_target_pairs={{1,0},{2,1},{3,2},{4,3},{5,4},{6,5},{7,6},{9,8},{10,9},{11,10},{12... | collective-permute-start | bytes 6291464 | tf_op jit(solution)/shard_map/ppermute | solution.py:512
  140.5 25.6 %collective-permute-start.22 = (bf16[8,128,1024]{2,1,0:T(8,128)(2,1)}, bf16[8,128,1024]{2,1,0:T(8,128)(2,1)S(1)}, u32[]{:S(2)}, u32[]{:S(2)}) collective-permute-start(bf16[8,128,1024]{2,1,0:T(8,128)(2,1)} %get-tuple-element.53), channel_id=1, source_target_pairs={{3,7},{4,0},{11,15},{12,8},{19,23},{20,16},{27,31},{28,24}} | collective-permute-start | bytes 6291464 | tf_op jit(solution)/shard_map/ppermute | solution.py:517
  141.3 27.2 %collective-permute-start.21 = (bf16[8,128,1024]{2,1,0:T(8,128)(2,1)}, bf16[8,128,1024]{2,1,0:T(8,128)(2,1)S(1)}, u32[]{:S(2)}, u32[]{:S(2)}) collective-permute-start(bf16[8,128,1024]{2,1,0:T(8,128)(2,1)} %get-tuple-element.52), channel_id=1, source_target_pairs={{3,4},{4,3},{11,12},{12,11},{19,20},{20,19},{27,28},{28,27}} | collective-permute-start | bytes 6291464 | tf_op jit(solution)/shard_map/ppermute | solution.py:514
  142.1 98.6 %collective-permute-start.8 = (bf16[12,128,1024]{2,1,0:T(8,128)(2,1)}, bf16[12,128,1024]{2,1,0:T(8,128)(2,1)}, u32[]{:S(2)}, u32[]{:S(2)}) collective-permute-start(bf16[12,128,1024]{2,1,0:T(8,128)(2,1)} %get-tuple-element.41), channel_id=1, source_target_pairs={{3,7},{4,0},{11,15},{12,8},{19,23},{20,16},{27,31},{28,24}} | collective-permute-start | bytes 9437192 | tf_op jit(solution)/shard_map/ppermute | solution.py:517
  164.2 21.1 %copy-start.4 = (bf16[8,128,1024]{2,1,0:T(8,128)(2,1)}, bf16[8,128,1024]{2,1,0:T(8,128)(2,1)S(1)}, u32[]{:S(2)}) copy-start(bf16[8,128,1024]{2,1,0:T(8,128)(2,1)S(1)} %collective-permute-done.3.high_ref) | copy-start | bytes 6291460
  164.2 148.4 %collective-permute-start.12 = (bf16[16,128,1024]{2,1,0:T(8,128)(2,1)}, bf16[16,128,1024]{2,1,0:T(8,128)(2,1)}, u32[]{:S(2)}, u32[]{:S(2)}) collective-permute-start(bf16[16,128,1024]{2,1,0:T(8,128)(2,1)} %get-tuple-element.44.tail_ref), channel_id=1, source_target_pairs={{0,1},{1,2},{2,3},{4,5},{5,6},{6,7},{8,9},{9,10},{10,11},{12,13},{... | collective-permute-start | bytes 12582920 | tf_op jit(solution)/shard_map/ppermute | solution.py:509
  166.2 146.5 %copy-start.29 = (bf16[8,128,1024]{2,1,0:T(8,128)(2,1)}, bf16[8,128,1024]{2,1,0:T(8,128)(2,1)S(1)}, u32[]{:S(2)}) copy-start(bf16[8,128,1024]{2,1,0:T(8,128)(2,1)S(1)} %collective-permute-done.22) | copy-start | bytes 6291460
  166.2 76.9 %collective-permute-start.15 = (bf16[12,128,1024]{2,1,0:T(8,128)(2,1)}, bf16[12,128,1024]{2,1,0:T(8,128)(2,1)}, u32[]{:S(2)}, u32[]{:S(2)}) collective-permute-start(bf16[12,128,1024]{2,1,0:T(8,128)(2,1)} %get-tuple-element.47), channel_id=1, source_target_pairs={{3,7},{4,0},{11,15},{12,8},{19,23},{20,16},{27,31},{28,24}} | collective-permute-start | bytes 9437192 | tf_op jit(solution)/shard_map/ppermute | solution.py:517
  168.5 163.1 %collective-permute-start.13 = (bf16[16,128,1024]{2,1,0:T(8,128)(2,1)}, bf16[16,128,1024]{2,1,0:T(8,128)(2,1)}, u32[]{:S(2)}, u32[]{:S(2)}) collective-permute-start(bf16[16,128,1024]{2,1,0:T(8,128)(2,1)} %get-tuple-element.45.head_ref), channel_id=1, source_target_pairs={{1,0},{2,1},{3,2},{5,4},{6,5},{7,6},{9,8},{10,9},{11,10},{13,12},{... | collective-permute-start | bytes 12582920 | tf_op jit(solution)/shard_map/ppermute | solution.py:512
  185.4 123.6 %collective-permute-start.7 = (bf16[12,128,1024]{2,1,0:T(8,128)(2,1)S(1)}, bf16[12,128,1024]{2,1,0:T(8,128)(2,1)S(1)}, u32[]{:S(2)}, u32[]{:S(2)}) collective-permute-start(bf16[12,128,1024]{2,1,0:T(8,128)(2,1)S(1)} %copy-done), channel_id=1, source_target_pairs={{1,0},{2,1},{3,2},{5,4},{6,5},{7,6},{9,8},{10,9},{11,10},{13,12},{... | collective-permute-start | bytes 9437192 | tf_op jit(solution)/shard_map/ppermute | solution.py:512
  240.7 92.9 %collective-permute-start.9 = (bf16[12,128,1024]{2,1,0:T(8,128)(2,1)}, bf16[12,128,1024]{2,1,0:T(8,128)(2,1)}, u32[]{:S(2)}, u32[]{:S(2)}) collective-permute-start(bf16[12,128,1024]{2,1,0:T(8,128)(2,1)} %collective-permute-done.8), channel_id=1, source_target_pairs={{7,4},{0,3},{15,12},{8,11},{23,20},{16,19},{31,28},{24,27}} | collective-permute-start | bytes 9437192 | tf_op jit(solution)/shard_map/ppermute | solution.py:520
  243.1 94.8 %collective-permute-start.16 = (bf16[12,128,1024]{2,1,0:T(8,128)(2,1)}, bf16[12,128,1024]{2,1,0:T(8,128)(2,1)}, u32[]{:S(2)}, u32[]{:S(2)}) collective-permute-start(bf16[12,128,1024]{2,1,0:T(8,128)(2,1)} %collective-permute-done.15), channel_id=1, source_target_pairs={{7,4},{0,3},{15,12},{8,11},{23,20},{16,19},{31,28},{24,27}} | collective-permute-start | bytes 9437192 | tf_op jit(solution)/shard_map/ppermute | solution.py:520
  310.8 118.3 %collective-permute-start.19 = (bf16[16,128,1024]{2,1,0:T(8,128)(2,1)}, bf16[16,128,1024]{2,1,0:T(8,128)(2,1)}, u32[]{:S(2)}, u32[]{:S(2)}) collective-permute-start(bf16[16,128,1024]{2,1,0:T(8,128)(2,1)} %get-tuple-element.50.tail_ref), channel_id=1, source_target_pairs={{0,1},{1,2},{2,3},{4,5},{5,6},{6,7},{8,9},{9,10},{10,11},{12,13},{... | collective-permute-start | bytes 12582920 | tf_op jit(solution)/shard_map/ppermute | solution.py:509
  312.7 27.1 %copy-start.28 = (f32[192]{0:T(256)S(1)}, f32[192]{0:T(256)}, u32[]{:S(2)}) copy-start(f32[192]{0:T(256)} %get-tuple-element.69) | copy-start | bytes 2308
  312.7 27.1 %copy-start.27 = (f32[192]{0:T(256)S(1)}, f32[192]{0:T(256)}, u32[]{:S(2)}) copy-start(f32[192]{0:T(256)} %param.7) | copy-start | bytes 2308
  312.7 118.7 %collective-permute-start.20 = (bf16[16,128,1024]{2,1,0:T(8,128)(2,1)}, bf16[16,128,1024]{2,1,0:T(8,128)(2,1)}, u32[]{:S(2)}, u32[]{:S(2)}) collective-permute-start(bf16[16,128,1024]{2,1,0:T(8,128)(2,1)} %get-tuple-element.51.head_ref), channel_id=1, source_target_pairs={{1,0},{2,1},{3,2},{5,4},{6,5},{7,6},{9,8},{10,9},{11,10},{13,12},{... | collective-permute-start | bytes 12582920 | tf_op jit(solution)/shard_map/ppermute | solution.py:512
  331.6 97.2 %collective-permute-start.26 = (bf16[12,128,1024]{2,1,0:T(8,128)(2,1)}, bf16[12,128,1024]{2,1,0:T(8,128)(2,1)S(1)}, u32[]{:S(2)}, u32[]{:S(2)}) collective-permute-start(bf16[12,128,1024]{2,1,0:T(8,128)(2,1)} %get-tuple-element.56.tail_ref), channel_id=1, source_target_pairs={{0,1},{1,2},{2,3},{3,4},{4,5},{5,6},{6,7},{8,9},{9,10},{10,11},{11... | collective-permute-start | bytes 9437192 | tf_op jit(solution)/shard_map/ppermute | solution.py:509
  333.7 113.0 %collective-permute-start.27 = (bf16[12,128,1024]{2,1,0:T(8,128)(2,1)}, bf16[12,128,1024]{2,1,0:T(8,128)(2,1)}, u32[]{:S(2)}, u32[]{:S(2)}) collective-permute-start(bf16[12,128,1024]{2,1,0:T(8,128)(2,1)} %get-tuple-element.57.head_ref), channel_id=1, source_target_pairs={{1,0},{2,1},{3,2},{4,3},{5,4},{6,5},{7,6},{9,8},{10,9},{11,10},{12... | collective-permute-start | bytes 9437192 | tf_op jit(solution)/shard_map/ppermute | solution.py:512
  337.9 94.8 %collective-permute-start.23 = (bf16[8,128,1024]{2,1,0:T(8,128)(2,1)}, bf16[8,128,1024]{2,1,0:T(8,128)(2,1)}, u32[]{:S(2)}, u32[]{:S(2)}) collective-permute-start(bf16[8,128,1024]{2,1,0:T(8,128)(2,1)} %copy-done.29), channel_id=1, source_target_pairs={{7,4},{0,3},{15,12},{8,11},{23,20},{16,19},{31,28},{24,27}} | collective-permute-start | bytes 6291464 | tf_op jit(solution)/shard_map/ppermute | solution.py:520
  361.3 67.5 %copy-start.11 = (f32[24,192]{1,0:T(8,128)S(1)}, f32[24,192]{1,0:T(8,128)}, u32[]{:S(2)}) copy-start(f32[24,192]{1,0:T(8,128)} %get-tuple-element.65.refs_0_) | copy-start | bytes 55300
  428.8 17.9 %copy-start.2 = (bf16[12,128,1024]{2,1,0:T(8,128)(2,1)}, bf16[12,128,1024]{2,1,0:T(8,128)(2,1)S(1)}, u32[]{:S(2)}) copy-start(bf16[12,128,1024]{2,1,0:T(8,128)(2,1)S(1)} %collective-permute-done.26.low_ref) | copy-start | bytes 9437188
  428.8 19.2 %collective-permute-start.37 = (f32[24,192]{1,0:T(8,128)S(1)}, f32[24,192]{1,0:T(8,128)S(1)}, u32[]{:S(2)}, u32[]{:S(2)}) collective-permute-start(f32[24,192]{1,0:T(8,128)S(1)} %copy-done.11), channel_id=1, source_target_pairs={{0,8},{8,16},{16,24},{24,0},{1,9},{9,17},{17,25},{25,1},{2,10},{10... | collective-permute-start | bytes 55304 | tf_op jit(solution)/shard_map/ppermute | solution.py:539
  429.0 21.9 %collective-permute-start.38 = (f32[24,192]{1,0:T(8,128)S(1)}, f32[24,192]{1,0:T(8,128)S(1)}, u32[]{:S(2)}, u32[]{:S(2)}) collective-permute-start(f32[24,192]{1,0:T(8,128)S(1)} %copy-done.11), channel_id=1, source_target_pairs={{0,16},{8,24},{16,0},{24,8},{1,17},{9,25},{17,1},{25,9},{2,18},{10... | collective-permute-start | bytes 55304 | tf_op jit(solution)/shard_map/ppermute | solution.py:539
  431.4 19.5 %collective-permute-start.39 = (f32[24,192]{1,0:T(8,128)S(1)}, f32[24,192]{1,0:T(8,128)S(1)}, u32[]{:S(2)}, u32[]{:S(2)}) collective-permute-start(f32[24,192]{1,0:T(8,128)S(1)} %copy-done.11), channel_id=1, source_target_pairs={{0,24},{8,0},{16,8},{24,16},{1,25},{9,1},{17,9},{25,17},{2,26},{10... | collective-permute-start | bytes 55304 | tf_op jit(solution)/shard_map/ppermute | solution.py:539
  432.7 19.3 %collective-permute-start.34 = (f32[24,192]{1,0:T(8,128)}, f32[24,192]{1,0:T(8,128)S(1)}, u32[]{:S(2)}, u32[]{:S(2)}) collective-permute-start(f32[24,192]{1,0:T(8,128)} %get-tuple-element.63.refs_0_), channel_id=1, source_target_pairs={{0,8},{8,16},{16,24},{24,0},{1,9},{9,17},{17,25},{25,1},{2,10},{10... | collective-permute-start | bytes 55304 | tf_op jit(solution)/shard_map/ppermute | solution.py:539
  446.7 18.5 %collective-permute-start.35 = (f32[24,192]{1,0:T(8,128)S(1)}, f32[24,192]{1,0:T(8,128)S(1)}, u32[]{:S(2)}, u32[]{:S(2)}) collective-permute-start(f32[24,192]{1,0:T(8,128)S(1)} %copy-done.15), channel_id=1, source_target_pairs={{0,16},{8,24},{16,0},{24,8},{1,17},{9,25},{17,1},{25,9},{2,18},{10... | collective-permute-start | bytes 55304 | tf_op jit(solution)/shard_map/ppermute | solution.py:539
  448.0 17.8 %collective-permute-start.36 = (f32[24,192]{1,0:T(8,128)S(1)}, f32[24,192]{1,0:T(8,128)S(1)}, u32[]{:S(2)}, u32[]{:S(2)}) collective-permute-start(f32[24,192]{1,0:T(8,128)S(1)} %copy-done.15), channel_id=1, source_target_pairs={{0,24},{8,0},{16,8},{24,16},{1,25},{9,1},{17,9},{25,17},{2,26},{10... | collective-permute-start | bytes 55304 | tf_op jit(solution)/shard_map/ppermute | solution.py:539
  450.9 16.4 %collective-permute-start.31 = (f32[24,192]{1,0:T(8,128)}, f32[24,192]{1,0:T(8,128)S(1)}, u32[]{:S(2)}, u32[]{:S(2)}) collective-permute-start(f32[24,192]{1,0:T(8,128)} %get-tuple-element.61.refs_0_), channel_id=1, source_target_pairs={{0,8},{8,16},{16,24},{24,0},{1,9},{9,17},{17,25},{25,1},{2,10},{10... | collective-permute-start | bytes 55304 | tf_op jit(solution)/shard_map/ppermute | solution.py:539
  451.0 42.1 %collective-permute-start.32 = (f32[24,192]{1,0:T(8,128)}, f32[24,192]{1,0:T(8,128)S(1)}, u32[]{:S(2)}, u32[]{:S(2)}) collective-permute-start(f32[24,192]{1,0:T(8,128)} %get-tuple-element.61.refs_0_), channel_id=1, source_target_pairs={{0,16},{8,24},{16,0},{24,8},{1,17},{9,25},{17,1},{25,9},{2,18},{10... | collective-permute-start | bytes 55304 | tf_op jit(solution)/shard_map/ppermute | solution.py:539
  452.0 41.1 %collective-permute-start.33 = (f32[24,192]{1,0:T(8,128)}, f32[24,192]{1,0:T(8,128)S(1)}, u32[]{:S(2)}, u32[]{:S(2)}) collective-permute-start(f32[24,192]{1,0:T(8,128)} %get-tuple-element.61.refs_0_), channel_id=1, source_target_pairs={{0,24},{8,0},{16,8},{24,16},{1,25},{9,1},{17,9},{25,17},{2,26},{10... | collective-permute-start | bytes 55304 | tf_op jit(solution)/shard_map/ppermute | solution.py:539
  465.3 37.2 %collective-permute-start.28 = (f32[16,192]{1,0:T(8,128)}, f32[16,192]{1,0:T(8,128)S(1)}, u32[]{:S(2)}, u32[]{:S(2)}) collective-permute-start(f32[16,192]{1,0:T(8,128)} %get-tuple-element.59.refs_0_), channel_id=1, source_target_pairs={{0,8},{8,16},{16,24},{24,0},{1,9},{9,17},{17,25},{25,1},{2,10},{10... | collective-permute-start | bytes 36872 | tf_op jit(solution)/shard_map/ppermute | solution.py:539
  465.8 36.7 %collective-permute-start.29 = (f32[16,192]{1,0:T(8,128)}, f32[16,192]{1,0:T(8,128)S(1)}, u32[]{:S(2)}, u32[]{:S(2)}) collective-permute-start(f32[16,192]{1,0:T(8,128)} %get-tuple-element.59.refs_0_), channel_id=1, source_target_pairs={{0,16},{8,24},{16,0},{24,8},{1,17},{9,25},{17,1},{25,9},{2,18},{10... | collective-permute-start | bytes 36872 | tf_op jit(solution)/shard_map/ppermute | solution.py:539
  467.4 35.2 %collective-permute-start.30 = (f32[16,192]{1,0:T(8,128)}, f32[16,192]{1,0:T(8,128)S(1)}, u32[]{:S(2)}, u32[]{:S(2)}) collective-permute-start(f32[16,192]{1,0:T(8,128)} %get-tuple-element.59.refs_0_), channel_id=1, source_target_pairs={{0,24},{8,0},{16,8},{24,16},{1,25},{9,1},{17,9},{25,17},{2,26},{10... | collective-permute-start | bytes 36872 | tf_op jit(solution)/shard_map/ppermute | solution.py:539
  (22 other events, 170.5 us)

commit v2 on v1

--- a/solution.py
+++ b/solution.py
@@ -423,12 +423,12 @@
 
 
 CHUNKS = (8, 12, 16, 16, 12)
-RELAYED = (0, 12, 12, 8, 0)
+RELAYED = (0, 12, 12, 6, 0)
 SUMMED = (1, 2, 3, 4)
 ORDER = (
     "H0 H1 S0 U0",
-    "D0 H2 S1 H3",
-    "V1 U1 D1 S2",
+    "D0 H2 S1 U1",
+    "D1 V1 H3 S2",
     "V2 U2 D2 Q2",
     "X1 H4 S3 V3",
     "U3 D3 Q3 W0",

time: 513 us -> 618 us (1.20)
  waiting for transfers between devices: 160 us -> 323 us
  starting transfers between devices: 161 us -> 106 us
    ppermute x5, waiting for transfers between devices: 66.7 us -> 154 us  [body(): made[name] = lax.ppermute(tail, 'wall', neighbour_pairs(walls, 1, skip))]
    ppermute x5, waiting for transfers between devices: 83.2 us -> 140 us  [body(): made[name] = lax.ppermute(head, 'wall', neighbour_pairs(walls, -1, skip))]
    ppermute x5, starting transfers between devices: 71.4 us -> 17.7 us  [body(): made[name] = lax.ppermute(head, 'wall', neighbour_pairs(walls, -1, skip))]
    ppermute x10, waiting for transfers between devices: 10.5 us -> 29 us  [body(): made[name] = lax.ppermute(edge, 'span', pairs)]
  transfers between devices with their start and end apart: 40 -> 40, of which waited for: 7 -> 6; matrix products, arithmetic and copies ran while one was open for 3% -> 2% of each run, Pallas kernels for 31% -> 26%
where the time goes in v2:
time: 618 us; the launch traced here: 616 us
  waiting for transfers between devices  323 us (52%)
  Pallas kernels  170 us (28%)
  starting transfers between devices  106 us (17%)
  local copies, waits for them, and re-layouts  13.4 us (2%)
    ppermute x5, waiting for transfers between devices, body(): made[name] = lax.ppermute(tail, 'wall', neighbour_pairs(walls, 1, skip))  154 us
    ppermute x5, waiting for transfers between devices, body(): made[name] = lax.ppermute(head, 'wall', neighbour_pairs(walls, -1, skip))  140 us
    pallas_call x5, Pallas kernels, span_filter(): pl.pallas_call(functools.partial(span_kernel, blocks, direct), grid_spec=...  73.9 us
    pallas_call x5, Pallas kernels, wall_filter(): pl.pallas_call(functools.partial(wall_kernel, group, first, direct, relay...  57.3 us
    ppermute x10, starting transfers between devices, body(): made[name] = lax.ppermute(edge, 'span', pairs)  45.5 us
    pallas_call x5, Pallas kernels, rescale(): pl.pallas_call(functools.partial(scale_kernel, len(energies), first - off...  38.3 us
    ppermute x10, waiting for transfers between devices, body(): made[name] = lax.ppermute(edge, 'span', pairs)  29 us
    ppermute x5, starting transfers between devices, body(): made[name] = lax.ppermute(head, 'wall', neighbour_pairs(walls, -1, skip))  17.7 us
  transfers between devices with their start and end apart: 40, of which 6 were waited for; matrix products, arithmetic and copies ran while one was open for 2% of the time, Pallas kernels for 26%

profile of v2, /device:TPU:6, one launch (start us, length us, event | category | flops | bytes accessed | tf_op | source)
XLA Modules:
  0.0 615.9 jit_solution(13512391457818098878)
XLA Ops:
  0.6 1.9 fusion.17
  4.1 3.6 fusion.16
  9.4 2.2 collective-permute-start.11
  11.6 3.8 collective-permute-start.18
  17.0 3.1 fusion.15
  20.1 13.4 %collective-permute-done.10.left_ref = bf16[16,192,128]{2,1,0:T(8,128)(2,1)S(1)} collective-permute-done((bf16[16,192,128]{2,1,0:T(8,128)(2,1)}, bf16[16,192,128]{2,1,0:T(8,128)(2,1)S(1)}, u32[]{:S(2)}, u32[]{:S(2)}) %collective-permute-start.10) | collective-permute-done | bytes 786464 | tf_op jit(solution)/shard_map/ppermute | solution.py:501
  33.5 18.6 %collective-permute-start.5 = (bf16[12,192,128]{2,1,0:T(8,128)(2,1)}, bf16[12,192,128]{2,1,0:T(8,128)(2,1)}, u32[]{:S(2)}, u32[]{:S(2)}) collective-permute-start(bf16[12,192,128]{2,1,0:T(8,128)(2,1)} %get-tuple-element.72), channel_id=1, source_target_pairs={{8,0},{16,8},{24,16},{0,24},{9,1},{17,9},{25,17},{1,25},{10,2},{18... | collective-permute-start | bytes 1769480 | tf_op jit(solution)/shard_map/ppermute | solution.py:501
  53.3 13.9 %collective-permute-done.17.left_ref = bf16[16,192,128]{2,1,0:T(8,128)(2,1)S(1)} collective-permute-done((bf16[16,192,128]{2,1,0:T(8,128)(2,1)}, bf16[16,192,128]{2,1,0:T(8,128)(2,1)S(1)}, u32[]{:S(2)}, u32[]{:S(2)}) %collective-permute-start.17) | collective-permute-done | bytes 786464 | tf_op jit(solution)/shard_map/ppermute | solution.py:501
  67.2 15.3 %collective-permute-start.24 = (bf16[12,192,128]{2,1,0:T(8,128)(2,1)}, bf16[12,192,128]{2,1,0:T(8,128)(2,1)}, u32[]{:S(2)}, u32[]{:S(2)}) collective-permute-start(bf16[12,192,128]{2,1,0:T(8,128)(2,1)} %get-tuple-element.71), channel_id=1, source_target_pairs={{0,8},{8,16},{16,24},{24,0},{1,9},{9,17},{17,25},{25,1},{2,10},{10... | collective-permute-start | bytes 1769480 | tf_op jit(solution)/shard_map/ppermute | solution.py:501
  82.5 15.9 %span_filter.7 = (bf16[16,128,1024]{2,1,0:T(8,128)(2,1)}, bf16[16,128,1024]{2,1,0:T(8,128)(2,1)}, bf16[4,128,1024]{2,1,0:T(8,128)(2,1)}, bf16[12,128,1024]{2,1,0:T(8,128)(2,1)}) custom-call(s32[1]{0:T(128)} %bitcast.flag_ref, f32[192,256]{1,0:T(8,128)} %fusion.12.taps_ref, bf16[16,192,128]{2,1,0:T(8,128)(2,1)} %copy-done.7, ...), custom_call_target="tpu_custom_call" | custom-call | flops 2415919104 | bytes 15728640 | tf_op jit(solution)/shard_map/span_filter/pallas_call | solution.py:205
  100.1 15.9 %span_filter.8 = (bf16[16,128,1024]{2,1,0:T(8,128)(2,1)}, bf16[16,128,1024]{2,1,0:T(8,128)(2,1)}, bf16[10,128,1024]{2,1,0:T(8,128)(2,1)}, bf16[6,128,1024]{2,1,0:T(8,128)(2,1)}) custom-call(s32[1]{0:T(128)} %bitcast.flag_ref, f32[192,256]{1,0:T(8,128)} %fusion.12.taps_ref, bf16[16,192,128]{2,1,0:T(8,128)(2,1)} %copy-done.5, ...), custom_call_target="tpu_custom_call" | custom-call | flops 2415919104 | bytes 15728640 | tf_op jit(solution)/shard_map/span_filter/pallas_call | solution.py:205
  117.7 1.9 collective-permute-start.22
  119.5 12.4 %span_filter.5 = (bf16[8,128,1024]{2,1,0:T(8,128)(2,1)}, bf16[8,128,1024]{2,1,0:T(8,128)(2,1)}) custom-call(s32[1]{0:T(128)} %bitcast.flag_ref, f32[192,256]{1,0:T(8,128)} %fusion.12.taps_ref, bf16[8,192,128]{2,1,0:T(8,128)(2,1)} %collective-permute-done.left_ref, bf16[64,192,1024]{2,1,0:T(8,128)(2,1)} %field_ref.9, ...), custom_call_target="tpu_custom_call" | custom-call | flops 1207959552 | bytes 7864320 | tf_op jit(solution)/shard_map/span_filter/pallas_call | solution.py:205
  131.9 1.9 collective-permute-start.25
  133.8 15.3 %span_filter.6 = (bf16[12,128,1024]{2,1,0:T(8,128)(2,1)}, bf16[12,128,1024]{2,1,0:T(8,128)(2,1)}, bf16[12,128,1024]{2,1,0:T(8,128)(2,1)}) custom-call(s32[1]{0:T(128)} %bitcast.flag_ref, f32[192,256]{1,0:T(8,128)} %fusion.12.taps_ref, bf16[12,192,128]{2,1,0:T(8,128)(2,1)} %collective-permute-done.4.left_ref, bf16[64,192,1024]{2,1,0:T(8,128)(2,1)} %field_ref.9, ...), custom_call_target="tpu_custom_call" | custom-call | flops 1811939328 | bytes 11796480 | tf_op jit(solution)/shard_map/span_filter/pallas_call | solution.py:205
  149.1 1.9 collective-permute-start.6
  151.0 1.9 collective-permute-start.2
  153.8 3.6 collective-permute-start.3
  157.4 2.3 collective-permute-start.8
  159.8 99.7 %collective-permute-done.2.low_ref = bf16[8,128,1024]{2,1,0:T(8,128)(2,1)S(1)} collective-permute-done((bf16[8,128,1024]{2,1,0:T(8,128)(2,1)}, bf16[8,128,1024]{2,1,0:T(8,128)(2,1)S(1)}, u32[]{:S(2)}, u32[]{:S(2)}) %collective-permute-start.2) | collective-permute-done | bytes 2097184 | tf_op jit(solution)/shard_map/ppermute | solution.py:509
  259.5 1.9 collective-permute-start.12
  261.4 2.4 collective-permute-start.15
  263.8 3.6 collective-permute-start.13
  267.4 2.7 collective-permute-start.7
  270.1 2.4 collective-permute-start.9
  272.5 2.4 collective-permute-start.16
  274.8 140.0 %collective-permute-done.7.high_ref = bf16[12,128,1024]{2,1,0:T(8,128)(2,1)} collective-permute-done((bf16[12,128,1024]{2,1,0:T(8,128)(2,1)}, bf16[12,128,1024]{2,1,0:T(8,128)(2,1)}, u32[]{:S(2)}, u32[]{:S(2)}) %collective-permute-start.7) | collective-permute-done | bytes 3145760 | tf_op jit(solution)/shard_map/ppermute | solution.py:512
  414.8 1.9 collective-permute-start.19
  416.8 3.8 collective-permute-start.20
  420.6 14.5 %span_filter.9 = (bf16[12,128,1024]{2,1,0:T(8,128)(2,1)}, bf16[12,128,1024]{2,1,0:T(8,128)(2,1)}) custom-call(s32[1]{0:T(128)} %bitcast.flag_ref, f32[192,256]{1,0:T(8,128)} %fusion.12.taps_ref, bf16[12,192,128]{2,1,0:T(8,128)(2,1)} %collective-permute-done.24.left_ref, bf16[64,192,1024]{2,1,0:T(8,128)(2,1)} %field_ref.9, ...), custom_call_target="tpu_custom_call" | custom-call | flops 1811939328 | bytes 11796480 | tf_op jit(solution)/shard_map/span_filter/pallas_call | solution.py:205
  435.1 2.4 collective-permute-start.26
  437.5 3.9 collective-permute-start.27
  441.5 1.8 collective-permute-start.23
  446.4 6.9 %wall_filter.5 = (bf16[8,192,1024]{2,1,0:T(8,128)(2,1)}, f32[192,1024]{1,0:T(8,128)}, f32[192,128]{1,0:T(8,128)}) custom-call(s32[1]{0:T(128)} %bitcast.flag_ref, bf16[192,448]{1,0:T(8,128)(2,1)} %fusion.4.matrix_ref, f32[192,128]{1,0:T(8,128)} %broadcast_in_dim.21.decay_ref, f32[192,128]{1,0:T(8,128)} %broadcast_in_dim.22.gain_ref, f32[192,1024]{1,0:T(8,128)} %start_ref.3, ...), custom_call_target="tpu_custom_call" | custom-call | flops 1409286144 | bytes 12582912 | tf_op jit(solution)/shard_map/wall_filter/pallas_call | solution.py:323
  453.3 11.6 %wall_filter.6 = (bf16[12,192,1024]{2,1,0:T(8,128)(2,1)}, f32[192,1024]{1,0:T(8,128)}, f32[192,128]{1,0:T(8,128)}, f32[24,192]{1,0:T(8,128)}) custom-call(s32[1]{0:T(128)} %bitcast.flag_ref, bf16[192,448]{1,0:T(8,128)(2,1)} %fusion.4.matrix_ref, f32[192,128]{1,0:T(8,128)} %broadcast_in_dim.21.decay_ref, f32[192,128]{1,0:T(8,128)} %broadcast_in_dim.22.gain_ref, ...), custom_call_target="tpu_custom_call" | custom-call | flops 2113929216 | bytes 18874368 | tf_op jit(solution)/shard_map/wall_filter/pallas_call | solution.py:323
  464.9 13.6 %wall_filter.7 = (bf16[16,192,1024]{2,1,0:T(8,128)(2,1)}, f32[192,1024]{1,0:T(8,128)}, f32[192,128]{1,0:T(8,128)}, f32[24,192]{1,0:T(8,128)}) custom-call(s32[1]{0:T(128)} %bitcast.flag_ref, bf16[192,448]{1,0:T(8,128)(2,1)} %fusion.4.matrix_ref, f32[192,128]{1,0:T(8,128)} %broadcast_in_dim.21.decay_ref, f32[192,128]{1,0:T(8,128)} %broadcast_in_dim.22.gain_ref, ...), custom_call_target="tpu_custom_call" | custom-call | flops 2818572288 | bytes 25165824 | tf_op jit(solution)/shard_map/wall_filter/pallas_call | solution.py:323
  478.5 54.0 %collective-permute-done.26.low_ref = bf16[12,128,1024]{2,1,0:T(8,128)(2,1)S(1)} collective-permute-done((bf16[12,128,1024]{2,1,0:T(8,128)(2,1)}, bf16[12,128,1024]{2,1,0:T(8,128)(2,1)S(1)}, u32[]{:S(2)}, u32[]{:S(2)}) %collective-permute-start.26) | collective-permute-done | bytes 3145760 | tf_op jit(solution)/shard_map/ppermute | solution.py:509
  532.8 2.0 collective-permute-start.38
  536.9 14.9 %wall_filter.8 = (bf16[16,192,1024]{2,1,0:T(8,128)(2,1)}, f32[192,1024]{1,0:T(8,128)}, f32[192,128]{1,0:T(8,128)}, f32[24,192]{1,0:T(8,128)}) custom-call(s32[1]{0:T(128)} %bitcast.flag_ref, bf16[192,448]{1,0:T(8,128)(2,1)} %fusion.4.matrix_ref, f32[192,128]{1,0:T(8,128)} %broadcast_in_dim.21.decay_ref, f32[192,128]{1,0:T(8,128)} %broadcast_in_dim.22.gain_ref, ...), custom_call_target="tpu_custom_call" | custom-call | flops 2818572288 | bytes 25165824 | tf_op jit(solution)/shard_map/wall_filter/pallas_call | solution.py:323
  553.4 2.9 collective-permute-start.36
  557.3 2.9 collective-permute-start.33
  560.2 10.4 %wall_filter.9 = (bf16[12,192,1024]{2,1,0:T(8,128)(2,1)}, f32[192,1024]{1,0:T(8,128)}, f32[192,128]{1,0:T(8,128)}, f32[16,192]{1,0:T(8,128)}) custom-call(s32[1]{0:T(128)} %bitcast.flag_ref, bf16[192,448]{1,0:T(8,128)(2,1)} %fusion.4.matrix_ref, f32[192,128]{1,0:T(8,128)} %broadcast_in_dim.21.decay_ref, f32[192,128]{1,0:T(8,128)} %broadcast_in_dim.22.gain_ref, ...), custom_call_target="tpu_custom_call" | custom-call | flops 2113929216 | bytes 18874368 | tf_op jit(solution)/shard_map/wall_filter/pallas_call | solution.py:323
  572.7 2.8 collective-permute-start.30
  576.3 5.9 rescale.5.refs_4_
  582.2 7.4 %rescale.6.refs_4_ = f32[64,192,1024]{2,1,0:T(8,128)} custom-call(f32[192,128]{1,0:T(8,128)} %broadcast_in_dim.21.decay_ref, f32[192,128]{1,0:T(8,128)} %broadcast_in_dim.22.gain_ref, f32[192,128]{1,0:T(8,128)} %broadcast_in_dim.23.rms_ref, f32[192,1024]{1,0:T(8,128)} %get-tuple-element.37.start_ref, ...), custom_call_target="tpu_custom_call", output_to_operand_aliasing={{}: (9, {})} | custom-call | flops 9437184 | bytes 14155776 | tf_op jit(solution)/shard_map/rescale/pallas_call | solution.py:392
  589.6 8.8 %rescale.7.refs_4_ = f32[64,192,1024]{2,1,0:T(8,128)} custom-call(f32[192,128]{1,0:T(8,128)} %broadcast_in_dim.21.decay_ref, f32[192,128]{1,0:T(8,128)} %broadcast_in_dim.22.gain_ref, f32[192,128]{1,0:T(8,128)} %broadcast_in_dim.23.rms_ref, f32[192,1024]{1,0:T(8,128)} %get-tuple-element.42.start_ref, ...), custom_call_target="tpu_custom_call", output_to_operand_aliasing={{}: (9, {})} | custom-call | flops 12582912 | bytes 18874368 | tf_op jit(solution)/shard_map/rescale/pallas_call | solution.py:392
  599.1 8.8 %rescale.8.refs_4_ = f32[64,192,1024]{2,1,0:T(8,128)} custom-call(f32[192,128]{1,0:T(8,128)} %broadcast_in_dim.21.decay_ref, f32[192,128]{1,0:T(8,128)} %broadcast_in_dim.22.gain_ref, f32[192,128]{1,0:T(8,128)} %broadcast_in_dim.23.rms_ref, f32[192,1024]{1,0:T(8,128)} %get-tuple-element.48.start_ref, ...), custom_call_target="tpu_custom_call", output_to_operand_aliasing={{}: (9, {})} | custom-call | flops 12582912 | bytes 18874368 | tf_op jit(solution)/shard_map/rescale/pallas_call | solution.py:392
  608.5 7.4 %rescale.9 = f32[64,192,1024]{2,1,0:T(8,128)} custom-call(f32[192,128]{1,0:T(8,128)} %broadcast_in_dim.21.decay_ref, f32[192,128]{1,0:T(8,128)} %broadcast_in_dim.22.gain_ref, f32[192,128]{1,0:T(8,128)} %broadcast_in_dim.23.rms_ref, f32[192,1024]{1,0:T(8,128)} %get-tuple-element.54.start_ref, ...), custom_call_target="tpu_custom_call", output_to_operand_aliasing={{}: (9, {})} | custom-call | flops 9437184 | bytes 14155776 | tf_op jit(solution)/shard_map/rescale/pallas_call | solution.py:392
  (118 shorter events, 22.4 us)
Async XLA Ops:
  2.6 17.5 %collective-permute-start = (bf16[8,192,128]{2,1,0:T(8,128)(2,1)}, bf16[8,192,128]{2,1,0:T(8,128)(2,1)}, u32[]{:S(2)}, u32[]{:S(2)}) collective-permute-start(bf16[8,192,128]{2,1,0:T(8,128)(2,1)} %get-tuple-element.79), channel_id=1, source_target_pairs={{0,8},{8,16},{16,24},{24,0},{1,9},{9,17},{17,25},{25,1},{2,10},{10... | collective-permute-start | bytes 1179656 | tf_op jit(solution)/shard_map/ppermute | solution.py:501
  7.8 25.7 %collective-permute-start.10 = (bf16[16,192,128]{2,1,0:T(8,128)(2,1)}, bf16[16,192,128]{2,1,0:T(8,128)(2,1)S(1)}, u32[]{:S(2)}, u32[]{:S(2)}) collective-permute-start(bf16[16,192,128]{2,1,0:T(8,128)(2,1)} %get-tuple-element.77), channel_id=1, source_target_pairs={{0,8},{8,16},{16,24},{24,0},{1,9},{9,17},{17,25},{25,1},{2,10},{10... | collective-permute-start | bytes 2359304 | tf_op jit(solution)/shard_map/ppermute | solution.py:501
  9.4 43.5 %collective-permute-start.11 = (bf16[16,192,128]{2,1,0:T(8,128)(2,1)}, bf16[16,192,128]{2,1,0:T(8,128)(2,1)S(1)}, u32[]{:S(2)}, u32[]{:S(2)}) collective-permute-start(bf16[16,192,128]{2,1,0:T(8,128)(2,1)} %get-tuple-element.76), channel_id=1, source_target_pairs={{8,0},{16,8},{24,16},{0,24},{9,1},{17,9},{25,17},{1,25},{10,2},{18... | collective-permute-start | bytes 2359304 | tf_op jit(solution)/shard_map/ppermute | solution.py:501
  11.6 55.6 %collective-permute-start.17 = (bf16[16,192,128]{2,1,0:T(8,128)(2,1)}, bf16[16,192,128]{2,1,0:T(8,128)(2,1)S(1)}, u32[]{:S(2)}, u32[]{:S(2)}) collective-permute-start(bf16[16,192,128]{2,1,0:T(8,128)(2,1)} %get-tuple-element.75), channel_id=1, source_target_pairs={{0,8},{8,16},{16,24},{24,0},{1,9},{9,17},{17,25},{25,1},{2,10},{10... | collective-permute-start | bytes 2359304 | tf_op jit(solution)/shard_map/ppermute | solution.py:501
  11.6 86.8 %collective-permute-start.18 = (bf16[16,192,128]{2,1,0:T(8,128)(2,1)}, bf16[16,192,128]{2,1,0:T(8,128)(2,1)S(1)}, u32[]{:S(2)}, u32[]{:S(2)}) collective-permute-start(bf16[16,192,128]{2,1,0:T(8,128)(2,1)} %get-tuple-element.74), channel_id=1, source_target_pairs={{8,0},{16,8},{24,16},{0,24},{9,1},{17,9},{25,17},{1,25},{10,2},{18... | collective-permute-start | bytes 2359304 | tf_op jit(solution)/shard_map/ppermute | solution.py:501
  20.1 111.8 %collective-permute-start.4 = (bf16[12,192,128]{2,1,0:T(8,128)(2,1)}, bf16[12,192,128]{2,1,0:T(8,128)(2,1)}, u32[]{:S(2)}, u32[]{:S(2)}) collective-permute-start(bf16[12,192,128]{2,1,0:T(8,128)(2,1)} %get-tuple-element.73), channel_id=1, source_target_pairs={{0,8},{8,16},{16,24},{24,0},{1,9},{9,17},{17,25},{25,1},{2,10},{10... | collective-permute-start | bytes 1769480 | tf_op jit(solution)/shard_map/ppermute | solution.py:501
  33.5 49.0 %copy-start.7 = (bf16[16,192,128]{2,1,0:T(8,128)(2,1)}, bf16[16,192,128]{2,1,0:T(8,128)(2,1)S(1)}, u32[]{:S(2)}) copy-start(bf16[16,192,128]{2,1,0:T(8,128)(2,1)S(1)} %collective-permute-done.10.left_ref) | copy-start | bytes 2359300
  33.5 100.3 %collective-permute-start.5 = (bf16[12,192,128]{2,1,0:T(8,128)(2,1)}, bf16[12,192,128]{2,1,0:T(8,128)(2,1)}, u32[]{:S(2)}, u32[]{:S(2)}) collective-permute-start(bf16[12,192,128]{2,1,0:T(8,128)(2,1)} %get-tuple-element.72), channel_id=1, source_target_pairs={{8,0},{16,8},{24,16},{0,24},{9,1},{17,9},{25,17},{1,25},{10,2},{18... | collective-permute-start | bytes 1769480 | tf_op jit(solution)/shard_map/ppermute | solution.py:501
  52.9 29.6 %copy-start.8 = (bf16[16,192,128]{2,1,0:T(8,128)(2,1)}, bf16[16,192,128]{2,1,0:T(8,128)(2,1)S(1)}, u32[]{:S(2)}) copy-start(bf16[16,192,128]{2,1,0:T(8,128)(2,1)S(1)} %collective-permute-done.11.right_ref) | copy-start | bytes 2359300
  52.9 64.8 %collective-permute-start.1 = (bf16[8,192,128]{2,1,0:T(8,128)(2,1)S(1)}, bf16[8,192,128]{2,1,0:T(8,128)(2,1)}, u32[]{:S(2)}, u32[]{:S(2)}) collective-permute-start(bf16[8,192,128]{2,1,0:T(8,128)(2,1)S(1)} %get-tuple-element.78), channel_id=1, source_target_pairs={{8,0},{16,8},{24,16},{0,24},{9,1},{17,9},{25,17},{1,25},{10,2},{18... | collective-permute-start | bytes 1179656 | tf_op jit(solution)/shard_map/ppermute | solution.py:501
  67.2 31.2 %copy-start.5 = (bf16[16,192,128]{2,1,0:T(8,128)(2,1)}, bf16[16,192,128]{2,1,0:T(8,128)(2,1)S(1)}, u32[]{:S(2)}) copy-start(bf16[16,192,128]{2,1,0:T(8,128)(2,1)S(1)} %collective-permute-done.17.left_ref) | copy-start | bytes 2359300
  67.2 83.8 %collective-permute-start.24 = (bf16[12,192,128]{2,1,0:T(8,128)(2,1)}, bf16[12,192,128]{2,1,0:T(8,128)(2,1)}, u32[]{:S(2)}, u32[]{:S(2)}) collective-permute-start(bf16[12,192,128]{2,1,0:T(8,128)(2,1)} %get-tuple-element.71), channel_id=1, source_target_pairs={{0,8},{8,16},{16,24},{24,0},{1,9},{9,17},{17,25},{25,1},{2,10},{10... | collective-permute-start | bytes 1769480 | tf_op jit(solution)/shard_map/ppermute | solution.py:501
  98.4 55.4 %collective-permute-start.14 = (bf16[4,128,1024]{2,1,0:T(8,128)(2,1)}, bf16[4,128,1024]{2,1,0:T(8,128)(2,1)}, u32[]{:S(2)}, u32[]{:S(2)}) collective-permute-start(bf16[4,128,1024]{2,1,0:T(8,128)(2,1)} %get-tuple-element.46), channel_id=1, source_target_pairs={{3,4},{4,3},{11,12},{12,11},{19,20},{20,19},{27,28},{28,27}} | collective-permute-start | bytes 3145736 | tf_op jit(solution)/shard_map/ppermute | solution.py:514
  117.7 39.8 %collective-permute-start.22 = (bf16[6,128,1024]{2,1,0:T(8,128)(2,1)}, bf16[6,128,1024]{2,1,0:T(8,128)(2,1)}, u32[]{:S(2)}, u32[]{:S(2)}) collective-permute-start(bf16[6,128,1024]{2,1,0:T(8,128)(2,1)} %get-tuple-element.53), channel_id=1, source_target_pairs={{3,7},{4,0},{11,15},{12,8},{19,23},{20,16},{27,31},{28,24}} | collective-permute-start | bytes 4718600 | tf_op jit(solution)/shard_map/ppermute | solution.py:517
  131.9 21.0 %collective-permute-start.25 = (bf16[12,192,128]{2,1,0:T(8,128)(2,1)}, bf16[12,192,128]{2,1,0:T(8,128)(2,1)}, u32[]{:S(2)}, u32[]{:S(2)}) collective-permute-start(bf16[12,192,128]{2,1,0:T(8,128)(2,1)} %get-tuple-element.70), channel_id=1, source_target_pairs={{8,0},{16,8},{24,16},{0,24},{9,1},{17,9},{25,17},{1,25},{10,2},{18... | collective-permute-start | bytes 1769480 | tf_op jit(solution)/shard_map/ppermute | solution.py:501
  149.1 118.3 %collective-permute-start.6 = (bf16[12,128,1024]{2,1,0:T(8,128)(2,1)}, bf16[12,128,1024]{2,1,0:T(8,128)(2,1)S(1)}, u32[]{:S(2)}, u32[]{:S(2)}) collective-permute-start(bf16[12,128,1024]{2,1,0:T(8,128)(2,1)} %get-tuple-element.39.tail_ref), channel_id=1, source_target_pairs={{0,1},{1,2},{2,3},{4,5},{5,6},{6,7},{8,9},{9,10},{10,11},{12,13},{... | collective-permute-start | bytes 9437192 | tf_op jit(solution)/shard_map/ppermute | solution.py:509
  151.0 108.5 %collective-permute-start.2 = (bf16[8,128,1024]{2,1,0:T(8,128)(2,1)}, bf16[8,128,1024]{2,1,0:T(8,128)(2,1)S(1)}, u32[]{:S(2)}, u32[]{:S(2)}) collective-permute-start(bf16[8,128,1024]{2,1,0:T(8,128)(2,1)} %get-tuple-element.35.tail_ref), channel_id=1, source_target_pairs={{0,1},{1,2},{2,3},{3,4},{4,5},{5,6},{6,7},{8,9},{9,10},{10,11},{11... | collective-permute-start | bytes 6291464 | tf_op jit(solution)/shard_map/ppermute | solution.py:509
  152.9 110.8 %collective-permute-start.21 = (bf16[10,128,1024]{2,1,0:T(8,128)(2,1)}, bf16[10,128,1024]{2,1,0:T(8,128)(2,1)S(1)}, u32[]{:S(2)}, u32[]{:S(2)}) collective-permute-start(bf16[10,128,1024]{2,1,0:T(8,128)(2,1)} %get-tuple-element.52), channel_id=1, source_target_pairs={{3,4},{4,3},{11,12},{12,11},{19,20},{20,19},{27,28},{28,27}} | collective-permute-start | bytes 7864328 | tf_op jit(solution)/shard_map/ppermute | solution.py:514
  153.8 107.6 %collective-permute-start.3 = (bf16[8,128,1024]{2,1,0:T(8,128)(2,1)}, bf16[8,128,1024]{2,1,0:T(8,128)(2,1)S(1)}, u32[]{:S(2)}, u32[]{:S(2)}) collective-permute-start(bf16[8,128,1024]{2,1,0:T(8,128)(2,1)} %get-tuple-element.36.head_ref), channel_id=1, source_target_pairs={{1,0},{2,1},{3,2},{4,3},{5,4},{6,5},{7,6},{9,8},{10,9},{11,10},{12... | collective-permute-start | bytes 6291464 | tf_op jit(solution)/shard_map/ppermute | solution.py:512
  157.4 112.7 %collective-permute-start.8 = (bf16[12,128,1024]{2,1,0:T(8,128)(2,1)}, bf16[12,128,1024]{2,1,0:T(8,128)(2,1)}, u32[]{:S(2)}, u32[]{:S(2)}) collective-permute-start(bf16[12,128,1024]{2,1,0:T(8,128)(2,1)} %get-tuple-element.41), channel_id=1, source_target_pairs={{3,7},{4,0},{11,15},{12,8},{19,23},{20,16},{27,31},{28,24}} | collective-permute-start | bytes 9437192 | tf_op jit(solution)/shard_map/ppermute | solution.py:517
  259.5 157.3 %collective-permute-start.12 = (bf16[16,128,1024]{2,1,0:T(8,128)(2,1)}, bf16[16,128,1024]{2,1,0:T(8,128)(2,1)}, u32[]{:S(2)}, u32[]{:S(2)}) collective-permute-start(bf16[16,128,1024]{2,1,0:T(8,128)(2,1)} %get-tuple-element.44.tail_ref), channel_id=1, source_target_pairs={{0,1},{1,2},{2,3},{4,5},{5,6},{6,7},{8,9},{9,10},{10,11},{12,13},{... | collective-permute-start | bytes 12582920 | tf_op jit(solution)/shard_map/ppermute | solution.py:509
  261.4 11.1 %collective-permute-start.15 = (bf16[12,128,1024]{2,1,0:T(8,128)(2,1)}, bf16[12,128,1024]{2,1,0:T(8,128)(2,1)}, u32[]{:S(2)}, u32[]{:S(2)}) collective-permute-start(bf16[12,128,1024]{2,1,0:T(8,128)(2,1)} %get-tuple-element.47), channel_id=1, source_target_pairs={{3,7},{4,0},{11,15},{12,8},{19,23},{20,16},{27,31},{28,24}} | collective-permute-start | bytes 9437192 | tf_op jit(solution)/shard_map/ppermute | solution.py:517
  263.8 171.3 %collective-permute-start.13 = (bf16[16,128,1024]{2,1,0:T(8,128)(2,1)}, bf16[16,128,1024]{2,1,0:T(8,128)(2,1)}, u32[]{:S(2)}, u32[]{:S(2)}) collective-permute-start(bf16[16,128,1024]{2,1,0:T(8,128)(2,1)} %get-tuple-element.45.head_ref), channel_id=1, source_target_pairs={{1,0},{2,1},{3,2},{5,4},{6,5},{7,6},{9,8},{10,9},{11,10},{13,12},{... | collective-permute-start | bytes 12582920 | tf_op jit(solution)/shard_map/ppermute | solution.py:512
  267.4 167.7 %copy-start = (bf16[12,128,1024]{2,1,0:T(8,128)(2,1)}, bf16[12,128,1024]{2,1,0:T(8,128)(2,1)S(1)}, u32[]{:S(2)}) copy-start(bf16[12,128,1024]{2,1,0:T(8,128)(2,1)S(1)} %collective-permute-done.6.low_ref) | copy-start | bytes 9437188
  267.4 147.4 %collective-permute-start.7 = (bf16[12,128,1024]{2,1,0:T(8,128)(2,1)}, bf16[12,128,1024]{2,1,0:T(8,128)(2,1)}, u32[]{:S(2)}, u32[]{:S(2)}) collective-permute-start(bf16[12,128,1024]{2,1,0:T(8,128)(2,1)} %get-tuple-element.40.head_ref), channel_id=1, source_target_pairs={{1,0},{2,1},{3,2},{5,4},{6,5},{7,6},{9,8},{10,9},{11,10},{13,12},{... | collective-permute-start | bytes 9437192 | tf_op jit(solution)/shard_map/ppermute | solution.py:512
  270.1 167.4 %collective-permute-start.9 = (bf16[12,128,1024]{2,1,0:T(8,128)(2,1)}, bf16[12,128,1024]{2,1,0:T(8,128)(2,1)}, u32[]{:S(2)}, u32[]{:S(2)}) collective-permute-start(bf16[12,128,1024]{2,1,0:T(8,128)(2,1)} %collective-permute-done.8), channel_id=1, source_target_pairs={{7,4},{0,3},{15,12},{8,11},{23,20},{16,19},{31,28},{24,27}} | collective-permute-start | bytes 9437192 | tf_op jit(solution)/shard_map/ppermute | solution.py:520
  272.5 169.0 %collective-permute-start.16 = (bf16[12,128,1024]{2,1,0:T(8,128)(2,1)}, bf16[12,128,1024]{2,1,0:T(8,128)(2,1)}, u32[]{:S(2)}, u32[]{:S(2)}) collective-permute-start(bf16[12,128,1024]{2,1,0:T(8,128)(2,1)} %collective-permute-done.15), channel_id=1, source_target_pairs={{7,4},{0,3},{15,12},{8,11},{23,20},{16,19},{31,28},{24,27}} | collective-permute-start | bytes 9437192 | tf_op jit(solution)/shard_map/ppermute | solution.py:520
  414.8 120.0 %collective-permute-start.19 = (bf16[16,128,1024]{2,1,0:T(8,128)(2,1)}, bf16[16,128,1024]{2,1,0:T(8,128)(2,1)}, u32[]{:S(2)}, u32[]{:S(2)}) collective-permute-start(bf16[16,128,1024]{2,1,0:T(8,128)(2,1)} %get-tuple-element.50.tail_ref), channel_id=1, source_target_pairs={{0,1},{1,2},{2,3},{4,5},{5,6},{6,7},{8,9},{9,10},{10,11},{12,13},{... | collective-permute-start | bytes 12582920 | tf_op jit(solution)/shard_map/ppermute | solution.py:509
  416.8 26.6 %copy-start.25 = (f32[192]{0:T(256)S(1)}, f32[192]{0:T(256)}, u32[]{:S(2)}) copy-start(f32[192]{0:T(256)} %param.7) | copy-start | bytes 2308
  416.8 119.6 %collective-permute-start.20 = (bf16[16,128,1024]{2,1,0:T(8,128)(2,1)}, bf16[16,128,1024]{2,1,0:T(8,128)(2,1)}, u32[]{:S(2)}, u32[]{:S(2)}) collective-permute-start(bf16[16,128,1024]{2,1,0:T(8,128)(2,1)} %get-tuple-element.51.head_ref), channel_id=1, source_target_pairs={{1,0},{2,1},{3,2},{5,4},{6,5},{7,6},{9,8},{10,9},{11,10},{13,12},{... | collective-permute-start | bytes 12582920 | tf_op jit(solution)/shard_map/ppermute | solution.py:512
  435.1 97.3 %collective-permute-start.26 = (bf16[12,128,1024]{2,1,0:T(8,128)(2,1)}, bf16[12,128,1024]{2,1,0:T(8,128)(2,1)S(1)}, u32[]{:S(2)}, u32[]{:S(2)}) collective-permute-start(bf16[12,128,1024]{2,1,0:T(8,128)(2,1)} %get-tuple-element.56.tail_ref), channel_id=1, source_target_pairs={{0,1},{1,2},{2,3},{3,4},{4,5},{5,6},{6,7},{8,9},{9,10},{10,11},{11... | collective-permute-start | bytes 9437192 | tf_op jit(solution)/shard_map/ppermute | solution.py:509
  437.5 114.3 %collective-permute-start.27 = (bf16[12,128,1024]{2,1,0:T(8,128)(2,1)}, bf16[12,128,1024]{2,1,0:T(8,128)(2,1)}, u32[]{:S(2)}, u32[]{:S(2)}) collective-permute-start(bf16[12,128,1024]{2,1,0:T(8,128)(2,1)} %get-tuple-element.57.head_ref), channel_id=1, source_target_pairs={{1,0},{2,1},{3,2},{4,3},{5,4},{6,5},{7,6},{9,8},{10,9},{11,10},{12... | collective-permute-start | bytes 9437192 | tf_op jit(solution)/shard_map/ppermute | solution.py:512
  441.5 91.3 %collective-permute-start.23 = (bf16[6,128,1024]{2,1,0:T(8,128)(2,1)}, bf16[6,128,1024]{2,1,0:T(8,128)(2,1)}, u32[]{:S(2)}, u32[]{:S(2)}) collective-permute-start(bf16[6,128,1024]{2,1,0:T(8,128)(2,1)} %collective-permute-done.22), channel_id=1, source_target_pairs={{7,4},{0,3},{15,12},{8,11},{23,20},{16,19},{31,28},{24,27}} | collective-permute-start | bytes 4718600 | tf_op jit(solution)/shard_map/ppermute | solution.py:520
  464.9 67.6 %copy-start.9 = (f32[24,192]{1,0:T(8,128)S(1)}, f32[24,192]{1,0:T(8,128)}, u32[]{:S(2)}) copy-start(f32[24,192]{1,0:T(8,128)} %get-tuple-element.65.refs_0_) | copy-start | bytes 55300
  532.4 19.4 %copy-start.1 = (bf16[12,128,1024]{2,1,0:T(8,128)(2,1)}, bf16[12,128,1024]{2,1,0:T(8,128)(2,1)S(1)}, u32[]{:S(2)}) copy-start(bf16[12,128,1024]{2,1,0:T(8,128)(2,1)S(1)} %collective-permute-done.26.low_ref) | copy-start | bytes 9437188
  532.4 20.9 %collective-permute-start.37 = (f32[24,192]{1,0:T(8,128)S(1)}, f32[24,192]{1,0:T(8,128)S(1)}, u32[]{:S(2)}, u32[]{:S(2)}) collective-permute-start(f32[24,192]{1,0:T(8,128)S(1)} %copy-done.9), channel_id=1, source_target_pairs={{0,8},{8,16},{16,24},{24,0},{1,9},{9,17},{17,25},{25,1},{2,10},{10... | collective-permute-start | bytes 55304 | tf_op jit(solution)/shard_map/ppermute | solution.py:539
  532.8 23.4 %collective-permute-start.38 = (f32[24,192]{1,0:T(8,128)S(1)}, f32[24,192]{1,0:T(8,128)S(1)}, u32[]{:S(2)}, u32[]{:S(2)}) collective-permute-start(f32[24,192]{1,0:T(8,128)S(1)} %copy-done.9), channel_id=1, source_target_pairs={{0,16},{8,24},{16,0},{24,8},{1,17},{9,25},{17,1},{25,9},{2,18},{10... | collective-permute-start | bytes 55304 | tf_op jit(solution)/shard_map/ppermute | solution.py:539
  534.8 21.5 %collective-permute-start.39 = (f32[24,192]{1,0:T(8,128)S(1)}, f32[24,192]{1,0:T(8,128)S(1)}, u32[]{:S(2)}, u32[]{:S(2)}) collective-permute-start(f32[24,192]{1,0:T(8,128)S(1)} %copy-done.9), channel_id=1, source_target_pairs={{0,24},{8,0},{16,8},{24,16},{1,25},{9,1},{17,9},{25,17},{2,26},{10... | collective-permute-start | bytes 55304 | tf_op jit(solution)/shard_map/ppermute | solution.py:539
  536.3 21.0 %collective-permute-start.34 = (f32[24,192]{1,0:T(8,128)}, f32[24,192]{1,0:T(8,128)S(1)}, u32[]{:S(2)}, u32[]{:S(2)}) collective-permute-start(f32[24,192]{1,0:T(8,128)} %get-tuple-element.63.refs_0_), channel_id=1, source_target_pairs={{0,8},{8,16},{16,24},{24,0},{1,9},{9,17},{17,25},{25,1},{2,10},{10... | collective-permute-start | bytes 55304 | tf_op jit(solution)/shard_map/ppermute | solution.py:539
  551.9 18.7 %collective-permute-start.35 = (f32[24,192]{1,0:T(8,128)S(1)}, f32[24,192]{1,0:T(8,128)S(1)}, u32[]{:S(2)}, u32[]{:S(2)}) collective-permute-start(f32[24,192]{1,0:T(8,128)S(1)} %copy-done.13), channel_id=1, source_target_pairs={{0,16},{8,24},{16,0},{24,8},{1,17},{9,25},{17,1},{25,9},{2,18},{10... | collective-permute-start | bytes 55304 | tf_op jit(solution)/shard_map/ppermute | solution.py:539
  553.4 17.2 %copy-start.10 = (f32[24,192]{1,0:T(8,128)}, f32[24,192]{1,0:T(8,128)S(1)}, u32[]{:S(2)}) copy-start(f32[24,192]{1,0:T(8,128)S(1)} %collective-permute-done.37.refs_1_) | copy-start | bytes 55300
  553.4 17.8 %collective-permute-start.36 = (f32[24,192]{1,0:T(8,128)S(1)}, f32[24,192]{1,0:T(8,128)S(1)}, u32[]{:S(2)}, u32[]{:S(2)}) collective-permute-start(f32[24,192]{1,0:T(8,128)S(1)} %copy-done.13), channel_id=1, source_target_pairs={{0,24},{8,0},{16,8},{24,16},{1,25},{9,1},{17,9},{25,17},{2,26},{10... | collective-permute-start | bytes 55304 | tf_op jit(solution)/shard_map/ppermute | solution.py:539
  556.3 16.4 %collective-permute-start.31 = (f32[24,192]{1,0:T(8,128)}, f32[24,192]{1,0:T(8,128)S(1)}, u32[]{:S(2)}, u32[]{:S(2)}) collective-permute-start(f32[24,192]{1,0:T(8,128)} %get-tuple-element.61.refs_0_), channel_id=1, source_target_pairs={{0,8},{8,16},{16,24},{24,0},{1,9},{9,17},{17,25},{25,1},{2,10},{10... | collective-permute-start | bytes 55304 | tf_op jit(solution)/shard_map/ppermute | solution.py:539
  556.3 42.1 %collective-permute-start.32 = (f32[24,192]{1,0:T(8,128)}, f32[24,192]{1,0:T(8,128)S(1)}, u32[]{:S(2)}, u32[]{:S(2)}) collective-permute-start(f32[24,192]{1,0:T(8,128)} %get-tuple-element.61.refs_0_), channel_id=1, source_target_pairs={{0,16},{8,24},{16,0},{24,8},{1,17},{9,25},{17,1},{25,9},{2,18},{10... | collective-permute-start | bytes 55304 | tf_op jit(solution)/shard_map/ppermute | solution.py:539
  557.3 41.1 %collective-permute-start.33 = (f32[24,192]{1,0:T(8,128)}, f32[24,192]{1,0:T(8,128)S(1)}, u32[]{:S(2)}, u32[]{:S(2)}) collective-permute-start(f32[24,192]{1,0:T(8,128)} %get-tuple-element.61.refs_0_), channel_id=1, source_target_pairs={{0,24},{8,0},{16,8},{24,16},{1,25},{9,1},{17,9},{25,17},{2,26},{10... | collective-permute-start | bytes 55304 | tf_op jit(solution)/shard_map/ppermute | solution.py:539
  570.6 37.3 %collective-permute-start.28 = (f32[16,192]{1,0:T(8,128)}, f32[16,192]{1,0:T(8,128)S(1)}, u32[]{:S(2)}, u32[]{:S(2)}) collective-permute-start(f32[16,192]{1,0:T(8,128)} %get-tuple-element.59.refs_0_), channel_id=1, source_target_pairs={{0,8},{8,16},{16,24},{24,0},{1,9},{9,17},{17,25},{25,1},{2,10},{10... | collective-permute-start | bytes 36872 | tf_op jit(solution)/shard_map/ppermute | solution.py:539
  571.2 36.7 %collective-permute-start.29 = (f32[16,192]{1,0:T(8,128)}, f32[16,192]{1,0:T(8,128)S(1)}, u32[]{:S(2)}, u32[]{:S(2)}) collective-permute-start(f32[16,192]{1,0:T(8,128)} %get-tuple-element.59.refs_0_), channel_id=1, source_target_pairs={{0,16},{8,24},{16,0},{24,8},{1,17},{9,25},{17,1},{25,9},{2,18},{10... | collective-permute-start | bytes 36872 | tf_op jit(solution)/shard_map/ppermute | solution.py:539
  572.7 35.2 %collective-permute-start.30 = (f32[16,192]{1,0:T(8,128)}, f32[16,192]{1,0:T(8,128)S(1)}, u32[]{:S(2)}, u32[]{:S(2)}) collective-permute-start(f32[16,192]{1,0:T(8,128)} %get-tuple-element.59.refs_0_), channel_id=1, source_target_pairs={{0,24},{8,0},{16,8},{24,16},{1,25},{9,1},{17,9},{25,17},{2,26},{10... | collective-permute-start | bytes 36872 | tf_op jit(solution)/shard_map/ppermute | solution.py:539
  (18 other events, 142.2 us)
